TPU v7x, 32 devices: a whole 2x2x4 slice. The times are simulated.
32 devices in a mesh: gx: 4 (over x, core), gz: 8 (over z, y).
Axes of the slice: x: 2, y: 2, z: 4, core: 2. Of those that a mesh axis runs over, the one named last changes fastest.
Arguments:
- conserved: float32 [5, 16, 32, 128], P(None, 'gx', 'gz'), may hold values from -1.1 to 5.5, as said below
- jacobian: float32 [16, 32, 128], P('gx', 'gz'), may hold values from 0.5 to 2
- metric: float32 [3, 3, 16, 32, 128], P(None, None, 'gx', 'gz'), may hold values from -0.45 to 2.01, as said below
- x_master: int32 [8, 8, 32], P('gx', 'gz'), may hold values from 0 to 1, as said below
- x_flip: int32 [8, 8, 32], P('gx', 'gz'), may hold values from 0 to 7, as said below
- z_master: int32 [4, 16, 32], P('gx', 'gz'), may hold values from 0 to 1, as said below
- z_flip: int32 [4, 16, 32], P('gx', 'gz'), may hold values from 0 to 7, as said below
Outputs:
- rhs: float32 [5, 16, 32, 128], P(None, 'gx', 'gz')
Inputs may be any that keep to these rules, and one draw needn't show every extreme that they name: conserved[0] is at least 0.6, and the pressure 0.4 (conserved[4] - 0.5 |conserved[1:4]|^2 / conserved[0]) is at least 0.6. metric[g, g] lies between 0.49 and 2.01; every other entry has magnitude at most 0.45. `x_master`: rows 2 t and 2 t + 1 hold the faces on the lower and upper streamwise boundary of tile t; 1 marks that tile t holds the master side. Row 2 t + 1 equals 1 minus row 2 t + 2 (rows taken cyclically), so each face has exactly one master. `x_flip`: rows as in x_master; row 2 t + 1 equals row 2 t + 2 (rows taken cyclically). `z_master`: columns 2 t and 2 t + 1 hold the faces on the lower and upper spanwise boundary of tile t; 1 marks that tile t holds the master side. Column 2 t + 1 equals 1 minus column 2 t + 2 (taken cyclically). `z_flip`: columns as in z_master; column 2 t + 1 equals column 2 t + 2 (taken cyclically).
All inputs are finite; a program needn't handle non-finite values.
Results may differ from a plain program's by a relative error of at most 0.0003.
Values sent between devices are 32-bit elements; how exact they have to be, the bound alone decides.
No kernel may reach another device: no remote copies, remote signals or barrier semaphores. Data moves between devices by JAX's collectives and lax.ppermute only.
A program may use at most 64 MiB of HBM per device.

v0:
```python
import math

import jax
import jax.numpy as jnp
import numpy as np
from jax import lax
from jax.experimental import pallas as pl
from jax.experimental.pallas import tpu as pltpu
from jax.sharding import PartitionSpec as P

gamma_gas = 1.4
visc_coef = 0.1
prandtl = 0.72
lift = 6.0
heat_coef = visc_coef * gamma_gas / ((gamma_gas - 1.0) * prandtl)
vmem_bytes = 8 << 20
whole = pl.BlockSpec(memory_space=pltpu.VMEM)


def node_table():
    points = np.array([-1.0, -math.sqrt(0.2), math.sqrt(0.2), 1.0])
    scales = np.array([np.prod([points[i] - points[k] for k in range(4) if k != i]) for i in range(4)])
    table = np.zeros((4, 4))
    for i in range(4):
        for k in range(4):
            if i != k:
                table[i, k] = scales[i] / (scales[k] * (points[i] - points[k]))
        table[i, i] = -np.sum(table[i])
    return table


def weak_table():
    table = node_table()
    table[0, 0] += lift
    table[3, 3] -= lift
    return table


def rows_of(lanes):
    return lax.broadcasted_iota(jnp.int32, (8, lanes), 0)


def lanes_of(lanes):
    return lax.broadcasted_iota(jnp.int32, (8, lanes), 1)


def pick4(index, values):
    out = jnp.full(index.shape, values[3], jnp.float32)
    for k in (2, 1, 0):
        out = jnp.where(index == k, jnp.float32(values[k]), out)
    return out


def shift_weights(index, table):
    weights = {}
    for shift in range(-3, 4):
        weights[shift] = pick4(index, [table[j, j - shift] if 0 <= j - shift < 4 else 0.0 for j in range(4)])
    return weights


class Frame:
    def __init__(self, lanes):
        self.lanes = lanes
        row = rows_of(lanes)
        lane = lanes_of(lanes)
        self.row, self.lane = row, lane
        self.low_half = row < 4
        self.point_row = row % 4
        self.point_lane = lane % 4

    def deriv_weights(self):
        table = weak_table()
        self.weights_z = shift_weights(self.point_row, table)
        self.weights_y = shift_weights(self.point_lane, table)
        pair = lambda top, bottom: jnp.where(self.low_half, jnp.float32(top), jnp.float32(bottom))
        self.weights_x = [
            [
                pair(table[2 * t, 2 * s], table[2 * t + 1, 2 * s + 1]),
                pair(table[2 * t, 2 * s + 1], table[2 * t + 1, 2 * s]),
            ]
            for t in range(2)
            for s in range(2)
        ]

    def swap(self, tile):
        return pltpu.roll(tile, 4, 0)

    def deriv_x(self, pair):
        a, b = pair
        a2, b2 = self.swap(a), self.swap(b)
        w = self.weights_x
        return [
            w[2 * t][0] * a + w[2 * t][1] * a2 + w[2 * t + 1][0] * b + w[2 * t + 1][1] * b2
            for t in range(2)
        ]

    def deriv_rows(self, tile):
        out = self.weights_z[0] * tile
        for shift in (-3, -2, -1, 1, 2, 3):
            out = out + self.weights_z[shift] * pltpu.roll(tile, shift % 8, 0)
        return out

    def deriv_lanes(self, tile):
        out = self.weights_y[0] * tile
        for shift in (-3, -2, -1, 1, 2, 3):
            out = out + self.weights_y[shift] * pltpu.roll(tile, shift % self.lanes, 1)
        return out

    def face_x(self, pair):
        return jnp.where(self.low_half, pair[0], pair[1])

    def face_z(self, pair):
        side = jnp.where(self.low_half, 0, 3)
        index = side + 4 * (self.point_row % 2)
        return jnp.where(self.point_row < 2, sub_gather(pair[0], index), sub_gather(pair[1], index))

    def spread_z(self, face):
        upper = jnp.where(self.point_row == 3, 4, 0)
        inner = jnp.where(self.low_half, 0, 1)
        return [sub_gather(face, upper + inner + 2 * t) for t in range(2)]

    def sides(self, low, up):
        return jnp.where(self.low_half, jnp.float32(low), jnp.float32(up))

    def sign_lanes(self):
        return jnp.where(
            self.point_lane == 3, jnp.float32(lift), jnp.where(self.point_lane == 0, jnp.float32(-lift), 0.0)
        )

    def sign_rows(self):
        return jnp.where(
            self.point_row == 3, jnp.float32(lift), jnp.where(self.point_row == 0, jnp.float32(-lift), 0.0)
        )


def sub_gather(tile, index):
    return jnp.take_along_axis(tile, index, axis=0)


def lane_gather(tile, index):
    return jnp.take_along_axis(tile, index, axis=1)


def primitive(state):
    inverse = 1.0 / state[0]
    velocity = [state[1 + j] * inverse for j in range(3)]
    kinetic = state[1] * velocity[0] + state[2] * velocity[1] + state[3] * velocity[2]
    pressure = (gamma_gas - 1.0) * (state[4] - 0.5 * kinetic)
    return velocity, pressure, pressure * inverse


def combos(values, rows):
    w0, w1, w2, w3 = values
    m0, m1, m2 = rows
    return [
        w0 * m0,
        w1 * m1,
        w2 * m2,
        w0 * m1 + w1 * m0,
        w0 * m2 + w2 * m0,
        w1 * m2 + w2 * m1,
        w3 * m0,
        w3 * m1,
        w3 * m2,
    ]


def normal_flux(state, velocity, pressure, slopes, normal):
    m0, m1, m2 = normal
    speed = velocity[0] * m0 + velocity[1] * m1 + velocity[2] * m2
    spread = (visc_coef * 2.0 / 3.0) * (slopes[0] + slopes[1] + slopes[2])
    t00, t11, t22 = [2.0 * visc_coef * slopes[d] - spread for d in range(3)]
    t01, t02, t12 = [visc_coef * slopes[3 + d] for d in range(3)]
    stress = [
        t00 * m0 + t01 * m1 + t02 * m2,
        t01 * m0 + t11 * m1 + t12 * m2,
        t02 * m0 + t12 * m1 + t22 * m2,
    ]
    heat = heat_coef * (slopes[6] * m0 + slopes[7] * m1 + slopes[8] * m2)
    work = velocity[0] * stress[0] + velocity[1] * stress[1] + velocity[2] * stress[2]
    out = [state[0] * speed]
    for j in range(3):
        out.append(state[1 + j] * speed + pressure * normal[j] - stress[j])
    out.append((state[4] + pressure) * speed - work - heat)
    return out, speed, heat


def wave(speed, theta, normal_size):
    return jnp.abs(speed) + jnp.sqrt(gamma_gas * theta) * normal_size


def size_of(normal):
    return jnp.sqrt(normal[0] * normal[0] + normal[1] * normal[1] + normal[2] * normal[2])


def pack(frame, fields, low_ref, up_ref):
    fields = list(fields)
    if len(fields) % 2:
        fields.append(fields[-1])
    for g in range(len(fields) // 2):
        a, b = fields[2 * g], fields[2 * g + 1]
        low_ref[8 * g : 8 * g + 8, :] = jnp.where(frame.low_half, a, frame.swap(b))
        up_ref[8 * g : 8 * g + 8, :] = jnp.where(frame.low_half, frame.swap(a), b)


def unpack(frame, left_ref, right_ref, count):
    fields = []
    for g in range((count + 1) // 2):
        left = left_ref[8 * g : 8 * g + 8, :]
        right = right_ref[8 * g : 8 * g + 8, :]
        fields.append(jnp.where(frame.low_half, left, frame.swap(right)))
        fields.append(jnp.where(frame.low_half, frame.swap(left), right))
    return fields[:count]


def spread_flags(frame, flags):
    count = flags.shape[-1]
    hit = lax.broadcasted_iota(jnp.int32, (count, frame.lanes), 0) == (
        lax.broadcasted_iota(jnp.int32, (count, frame.lanes), 1) // 4
    )
    wide = jnp.dot(
        flags.astype(jnp.float32), hit.astype(jnp.float32), preferred_element_type=jnp.float32
    )
    wide = (wide + 0.5).astype(jnp.int32)
    shape = (8, frame.lanes)
    return jnp.where(
        frame.low_half, jnp.broadcast_to(wide[0:1], shape), jnp.broadcast_to(wide[1:2], shape)
    )


def turn_indices(frame, code, forward_low):
    swap = (code & 4) != 0
    first = (code & 1) * 3
    second = ((code >> 1) & 1) * 3
    forward = frame.low_half if forward_low else jnp.logical_not(frame.low_half)
    flip_a = jnp.where(forward, second, first)
    flip_b = jnp.where(forward, first, second)
    row4, lane4 = frame.point_row, frame.point_lane
    lane_base = frame.lane - lane4
    row_base = frame.row - row4
    step1 = lane_base + jnp.where(swap, (lane4 - row4) & 3, lane4)
    step2 = row_base + jnp.where(swap, (lane4 - (row4 ^ flip_b)) & 3, row4 ^ first)
    step3 = lane_base + jnp.where(swap, ((lane4 ^ flip_a) + (row4 ^ flip_b)) & 3, lane4 ^ second)
    return step1, step2, step3


def turn(tile, indices):
    return lane_gather(sub_gather(lane_gather(tile, indices[0]), indices[1]), indices[2])


def load_pair(ref, f):
    return [ref[f, 0:8, :], ref[f, 8:16, :]]


def load_state(ref):
    pairs = [load_pair(ref, f) for f in range(5)]
    return [[pairs[f][t] for f in range(5)] for t in range(2)]


def load_rows(ref, g):
    pairs = [load_pair(ref, 3 * g + d) for d in range(3)]
    return [[pairs[d][t] for d in range(3)] for t in range(2)]


def by_field(tiles):
    return [[tiles[0][f], tiles[1][f]] for f in range(len(tiles[0]))]


def lane_partner(frame, tile, flip):
    before = pltpu.roll(tile, 1, 1)
    after = pltpu.roll(tile, frame.lanes - 1, 1)
    other = jnp.where(frame.point_lane == 3, after, before)
    wall = (frame.lane == 0) | (frame.lane == frame.lanes - 1)
    return jnp.where(wall, -tile if flip else tile, other)


def lane_normal(frame, rows):
    take_before = (frame.point_lane == 0) & (frame.lane != 0)
    return [jnp.where(take_before, pltpu.roll(r, 1, 1), r) for r in rows]


def first_kernel(cons, jac, met, xm_ref, xf_ref, grad_out, turned_out, low_out, up_out):
    frame = Frame(cons.shape[-1])
    frame.deriv_weights()
    state = load_state(cons)
    rows = [load_rows(met, g) for g in range(3)]
    lifted = []
    for t in range(2):
        velocity, _, theta = primitive(state[t])
        lifted.append(velocity + [theta])
    cx = by_field([combos(lifted[t], rows[0][t]) for t in range(2)])
    cz = by_field([combos(lifted[t], rows[1][t]) for t in range(2)])
    cy = by_field([combos(lifted[t], rows[2][t]) for t in range(2)])
    sign = frame.sign_lanes()
    lane_part = []
    for t in range(2):
        other = [lane_partner(frame, lifted[t][k], k < 3) for k in range(4)]
        mean = [0.5 * (lifted[t][k] + other[k]) for k in range(4)]
        lane_part.append(combos(mean, lane_normal(frame, rows[2][t])))
    grad = []
    for f in range(9):
        dx = frame.deriv_x(cx[f])
        grad.append(
            [
                dx[t]
                + frame.deriv_rows(cz[f][t])
                + frame.deriv_lanes(cy[f][t])
                + sign * lane_part[t][f]
                for t in range(2)
            ]
        )
    for f in range(9):
        for t in range(2):
            grad_out[f, 8 * t : 8 * t + 8, :] = grad[f][t]

    inverse = [1.0 / jac[0:8, :], 1.0 / jac[8:16, :]]
    state_f = by_field(state)
    code = spread_flags(frame, xf_ref[...])
    lead = spread_flags(frame, xm_ref[...]) == 1
    indices = turn_indices(frame, code, True)
    own_x = [frame.face_x(p) for p in state_f + by_field(rows[0])]
    turned = [turn(p, indices) for p in own_x + [frame.face_x(inverse)]]
    for f in range(9):
        turned_out[8 * f : 8 * f + 8, :] = turned[f]
    velocity, _, theta = primitive(turned[:5])
    line = velocity + [theta]
    outer = (frame.point_row == 0) | (frame.point_row == 3)
    pick = jnp.where(frame.low_half, 0, 3) + jnp.where(frame.point_row >= 2, 4, 0)
    merge = lambda a, b: jnp.where(outer, sub_gather(a, pick), sub_gather(b, pick))
    zero = jnp.zeros_like(line[0])
    edges = [merge(line[0], line[1]), merge(line[2], line[3])]
    for d in range(3):
        edges.append(
            merge(jnp.where(lead, turned[5 + d], zero), jnp.where(lead, own_x[5 + d], zero))
        )
    faces = [frame.face_z(p) for p in state_f + by_field(rows[1]) + [inverse] + grad]
    pack(frame, faces + edges, low_out, up_out)


def second_kernel(
    cons, met, zm_ref, zf_ref, xf_ref, grad_in, turned_in, left, right, grad_out, low_out, up_out
):
    frame = Frame(cons.shape[-1])
    code = spread_flags(frame, zf_ref[...])
    lead = spread_flags(frame, zm_ref[...]) == 1
    indices = turn_indices(frame, code, False)
    got = unpack(frame, left, right, 23)
    other = [turn(p, indices) for p in got[:8]]
    own = [frame.face_z(load_pair(cons, f)) for f in range(5)]
    own_rows = [frame.face_z(load_pair(met, 3 + d)) for d in range(3)]
    velocity, _, theta = primitive(own)
    velocity2, _, theta2 = primitive(other[:5])
    mean = [0.5 * (a + b) for a, b in zip(velocity + [theta], velocity2 + [theta2])]
    normal = [jnp.where(lead, own_rows[d], other[5 + d]) for d in range(3)]
    part = combos(mean, normal)
    sign = frame.sign_rows()
    faces = []
    x_code = spread_flags(frame, xf_ref[...])
    x_indices = turn_indices(frame, x_code, True)
    for f in range(9):
        spread = frame.spread_z(part[f])
        total = [grad_in[f, 8 * t : 8 * t + 8, :] + sign * spread[t] for t in range(2)]
        for t in range(2):
            grad_out[f, 8 * t : 8 * t + 8, :] = total[t]
        faces.append(turn(frame.face_x(total), x_indices))
    turned = [turned_in[8 * f : 8 * f + 8, :] for f in range(9)]
    odd = frame.point_row % 2
    high = jnp.where(frame.point_row >= 2, 4, 0)
    both = high + jnp.where(frame.low_half, odd, 3 - odd)
    outer = high + jnp.where(frame.low_half, 0, 3)
    lines = [sub_gather(got[18], both), sub_gather(got[19], both)]
    lines.append(jnp.where(odd == 0, sub_gather(got[20], outer), sub_gather(got[21], outer)))
    lines.append(sub_gather(got[22], outer))
    pack(frame, turned + faces + lines, low_out, up_out)


def third_kernel(
    cons, jac, met, xm_ref, zm_ref, zf_ref, grad_in, left_z, right_z, left_x, right_x, out
):
    frame = Frame(cons.shape[-1])
    frame.deriv_weights()
    state = load_state(cons)
    state_f = by_field(state)
    rows = [load_rows(met, g) for g in range(3)]
    inverse = [1.0 / jac[0:8, :], 1.0 / jac[8:16, :]]
    prims = [primitive(state[t]) for t in range(2)]
    got_z = unpack(frame, left_z, right_z, 23)
    got_x = unpack(frame, left_x, right_x, 22)
    x_lead = spread_flags(frame, xm_ref[...]) == 1
    z_lead = spread_flags(frame, zm_ref[...]) == 1
    z_indices = turn_indices(frame, spread_flags(frame, zf_ref[...]), False)
    face_sign = frame.sides(-lift, lift)
    side_sign = frame.sides(-1.0, 1.0)

    own = [frame.face_x(p) for p in state_f]
    own_rows = [frame.face_x(p) for p in by_field(rows[0])]
    own_prim = primitive(own)
    other = got_x[:5]
    other_prim = primitive(other)
    normal_x = [jnp.where(x_lead, own_rows[d], got_x[5 + d]) for d in range(3)]
    mean = [
        0.5 * (a + b)
        for a, b in zip(own_prim[0] + [own_prim[2]], other_prim[0] + [other_prim[2]])
    ]
    part = combos(mean, normal_x)
    slopes = []
    for f in range(9):
        lifted_part = face_sign * part[f]
        zero = jnp.zeros_like(lifted_part)
        tiles = [
            grad_in[f, 0:8, :] + jnp.where(frame.low_half, lifted_part, zero),
            grad_in[f, 8:16, :] + jnp.where(frame.low_half, zero, lifted_part),
        ]
        slopes.append([tiles[t] * inverse[t] for t in range(2)])
    own_slopes = [frame.face_x(p) for p in slopes]
    other_slopes = [(got_x[9 + f] - face_sign * part[f]) * got_x[8] for f in range(9)]

    def face_flux(own, own_prim, own_slopes, other, other_prim, other_slopes, normal):
        size = size_of(normal)
        flux1, speed1, _ = normal_flux(own, own_prim[0], own_prim[1], own_slopes, normal)
        flux2, speed2, _ = normal_flux(other, other_prim[0], other_prim[1], other_slopes, normal)
        fastest = jnp.maximum(wave(speed1, own_prim[2], size), wave(speed2, other_prim[2], size))
        half = 0.5 * side_sign * fastest
        return [
            0.5 * (flux1[c] + flux2[c]) - half * (other[c] - own[c]) for c in range(5)
        ]

    flux_x = face_flux(own, own_prim, own_slopes, other, other_prim, other_slopes, normal_x)

    edge_a = jnp.where(frame.low_half, 0, 2) + jnp.where(frame.point_row >= 2, 4, 0)
    edge_b = edge_a + 1
    lines = [
        sub_gather(got_x[18], edge_a),
        sub_gather(got_x[18], edge_b),
        sub_gather(got_x[19], edge_a),
        sub_gather(got_x[19], edge_b),
    ]
    line_rows = [
        sub_gather(got_x[20], edge_a),
        sub_gather(got_x[20], edge_b),
        sub_gather(got_x[21], edge_a),
    ]
    own_edge = jnp.where(frame.low_half, 0, 4) + jnp.where(frame.point_row >= 2, 2, 1)
    line_rows = [line_rows[d] + sub_gather(got_z[20 + d], own_edge) for d in range(3)]
    raw_prim = primitive(got_z[:5])
    edge_mean = [0.5 * (a + b) for a, b in zip(raw_prim[0] + [raw_prim[2]], lines)]
    edge_part = combos(edge_mean, line_rows)
    edge_sign = frame.sign_rows()
    other_grad = [turn(got_z[9 + f] + edge_sign * edge_part[f], z_indices) for f in range(9)]
    turned = [turn(p, z_indices) for p in got_z[:9]]
    other = turned[:5]
    other_prim = primitive(other)
    own = [frame.face_z(p) for p in state_f]
    own_prim = primitive(own)
    own_rows = [frame.face_z(p) for p in by_field(rows[1])]
    normal_z = [jnp.where(z_lead, own_rows[d], turned[5 + d]) for d in range(3)]
    mean = [
        0.5 * (a + b)
        for a, b in zip(own_prim[0] + [own_prim[2]], other_prim[0] + [other_prim[2]])
    ]
    part = combos(mean, normal_z)
    other_slopes = [(other_grad[f] - face_sign * part[f]) * turned[8] for f in range(9)]
    own_slopes = [frame.face_z(p) for p in slopes]
    flux_z = face_flux(own, own_prim, own_slopes, other, other_prim, other_slopes, normal_z)

    slopes_t = [[slopes[f][t] for f in range(9)] for t in range(2)]
    sign_y = frame.sign_lanes()
    up_lane = frame.point_lane == 3
    wall = (frame.lane == 0) | (frame.lane == frame.lanes - 1)
    volume = []
    lane_flux = []
    for t in range(2):
        velocity, pressure, theta = prims[t]
        volume.append(
            [normal_flux(state[t], velocity, pressure, slopes_t[t], rows[g][t])[0] for g in range(3)]
        )
        normal = lane_normal(frame, rows[2][t])
        half, speed, heat = normal_flux(state[t], velocity, pressure, slopes_t[t], normal)
        own_wave = wave(speed, theta, size_of(normal))
        fastest = jnp.maximum(own_wave, lane_partner(frame, own_wave, False))
        mirrored = [-half[0], half[1], half[2], half[3], -half[4] - 2.0 * heat]
        direction = jnp.where(up_lane, jnp.float32(0.5), jnp.float32(-0.5)) * fastest
        result = []
        for c in range(5):
            other_half = jnp.where(wall, mirrored[c], lane_partner(frame, half[c], False))
            other_state = lane_partner(frame, state[t][c], 1 <= c <= 3)
            result.append(
                0.5 * (half[c] + other_half) - direction * (other_state - state[t][c])
            )
        lane_flux.append(result)
    row_sign = frame.sign_rows()
    for c in range(5):
        dx = frame.deriv_x([volume[t][0][c] for t in range(2)])
        spread = frame.spread_z(flux_z[c])
        side = face_sign * flux_x[c]
        zero = jnp.zeros_like(side)
        for t in range(2):
            total = (
                dx[t]
                + frame.deriv_rows(volume[t][1][c])
                + frame.deriv_lanes(volume[t][2][c])
                + sign_y * lane_flux[t][c]
                + row_sign * spread[t]
                + (jnp.where(frame.low_half, side, zero) if t == 0 else jnp.where(frame.low_half, zero, side))
            )
            out[c, 8 * t : 8 * t + 8, :] = -total * inverse[t]


def call(kernel, outs, *args):
    return pl.pallas_call(
        kernel,
        out_shape=[jax.ShapeDtypeStruct(s, jnp.float32) for s in outs],
        in_specs=[whole] * len(args),
        out_specs=[whole] * len(outs),
        compiler_params=pltpu.CompilerParams(vmem_limit_bytes=vmem_bytes),
    )(*args)


def exchange(low, up, axis):
    count = lax.axis_size(axis)
    from_left = lax.ppermute(up, axis, [(i, (i + 1) % count) for i in range(count)])
    from_right = lax.ppermute(low, axis, [((i + 1) % count, i) for i in range(count)])
    return from_left, from_right


def local(conserved, jacobian, metric, x_master, x_flip, z_master, z_flip):
    lanes = conserved.shape[-1]
    nodes = conserved.shape[1] * conserved.shape[2]
    assert conserved.shape[1:3] == (4, 4)
    cons = conserved.reshape(5, nodes, lanes)
    jac = jacobian.reshape(nodes, lanes)
    met = metric.reshape(9, nodes, lanes)
    xm, xf, zm, zf = [a.reshape(2, a.shape[-1]) for a in (x_master, x_flip, z_master, z_flip)]
    grad, turned, low_z, up_z = call(
        first_kernel,
        [(9, nodes, lanes), (72, lanes), (96, lanes), (96, lanes)],
        cons, jac, met, xm, xf,
    )
    left_z, right_z = exchange(low_z, up_z, "gz")
    grad, low_x, up_x = call(
        second_kernel,
        [(9, nodes, lanes), (88, lanes), (88, lanes)],
        cons, met, zm, zf, xf, grad, turned, left_z, right_z,
    )
    left_x, right_x = exchange(low_x, up_x, "gx")
    (rhs,) = call(
        third_kernel,
        [(5, nodes, lanes)],
        cons, jac, met, xm, zm, zf, grad, left_z, right_z, left_x, right_x,
    )
    return rhs.reshape(conserved.shape)


def solution(mesh):
    in_specs = (
        P(None, "gx", "gz", None),
        P("gx", "gz", None),
        P(None, None, "gx", "gz", None),
        P("gx", "gz", None),
        P("gx", "gz", None),
        P("gx", "gz", None),
        P("gx", "gz", None),
    )
    out_specs = P(None, "gx", "gz", None)
    return jax.shard_map(local, mesh=mesh, in_specs=in_specs, out_specs=out_specs, check_vma=False)
```

profile of v0, /device:TPU:1, one launch (start us, length us, event | category | flops | bytes accessed | tf_op | source)
XLA Modules:
  0.0 18.4 jit_solution(2496316236774066309)
XLA Ops:
  0.0 0.0 copy-start.3
  0.0 0.0 copy-start.4
  0.0 0.7 %copy-done.3 = f32[4,4,128]{2,1,0:T(4,128)S(1)} copy-done((f32[4,4,128]{2,1,0:T(4,128)S(1)}, f32[4,4,128]{2,1,0:T(4,128)}, u32[]{:S(2)}) %copy-start.3) | copy-done | bytes 8216
  0.7 0.0 copy-done.4
  0.7 0.0 copy-start
  0.7 0.9 %copy-done = f32[3,3,4,4,128]{4,3,2,1,0:T(4,128)S(1)} copy-done((f32[3,3,4,4,128]{4,3,2,1,0:T(4,128)S(1)}, f32[3,3,4,4,128]{4,3,2,1,0:T(4,128)}, u32[]{:S(2)}) %copy-start) | copy-done | bytes 73752
  1.6 0.0 copy-start.2
  1.6 0.8 %copy-done.2 = f32[5,4,4,128]{3,2,1,0:T(4,128)S(1)} copy-done((f32[5,4,4,128]{3,2,1,0:T(4,128)S(1)}, f32[5,4,4,128]{3,2,1,0:T(4,128)}, u32[]{:S(2)}) %copy-start.2) | copy-done | bytes 40984
  2.4 0.0 copy-start.5
  2.4 0.7 %copy-done.5 = s32[2,1,32]{2,1,0:T(1,128)S(1)} copy-done((s32[2,1,32]{2,1,0:T(1,128)S(1)}, s32[2,1,32]{2,1,0:T(1,128)}, u32[]{:S(2)}) %copy-start.5) | copy-done | bytes 280
  3.0 0.0 copy-start.1
  3.0 0.3 %shard_map.73 = (f32[9,16,128]{2,1,0:T(8,128)S(1)}, f32[72,128]{1,0:T(8,128)S(1)}, f32[96,128]{1,0:T(8,128)S(1)}, f32[96,128]{1,0:T(8,128)S(1)}) custom-call(f32[5,16,128]{2,1,0:T(8,128)S(1)} %bitcast.11, f32[16,128]{1,0:T(8,128)S(1)} %bitcast.14, f32[9,16,128]{2,1,0:T(8,128)S(1)} %bitcast.8, s32[2,32]{1,0:T(2,128)S(1)} %bitcast.18, s32[2,32]{1,0:T(2,128)S(1)} %bitcast.16), custom_call_target="tpu_custom_call" | custom-call | tf_op jit(solution)/shard_map/pallas_call | solution.py:510
  3.3 2.1 %collective-permute-start = (f32[96,128]{1,0:T(8,128)S(1)}, f32[96,128]{1,0:T(8,128)S(1)}, u32[]{:S(2)}, u32[]{:S(2)}) collective-permute-start(f32[96,128]{1,0:T(8,128)S(1)} %get-tuple-element.14), channel_id=1, source_target_pairs={{0,1},{1,2},{2,3},{3,4},{4,5},{5,6},{6,7},{7,0},{8,9},{9,10},{10,1... | collective-permute-start | bytes 147464 | tf_op jit(solution)/shard_map/ppermute | solution.py:521
  5.5 3.1 %collective-permute-start.1 = (f32[96,128]{1,0:T(8,128)S(1)}, f32[96,128]{1,0:T(8,128)S(1)}, u32[]{:S(2)}, u32[]{:S(2)}) collective-permute-start(f32[96,128]{1,0:T(8,128)S(1)} %get-tuple-element.15), channel_id=1, source_target_pairs={{1,0},{2,1},{3,2},{4,3},{5,4},{6,5},{7,6},{0,7},{9,8},{10,9},{11,1... | collective-permute-start | bytes 147464 | tf_op jit(solution)/shard_map/ppermute | solution.py:522
  8.6 1.5 %collective-permute-done.left.left_z = f32[96,128]{1,0:T(8,128)S(1)} collective-permute-done((f32[96,128]{1,0:T(8,128)S(1)}, f32[96,128]{1,0:T(8,128)S(1)}, u32[]{:S(2)}, u32[]{:S(2)}) %collective-permute-start) | collective-permute-done | bytes 49184 | tf_op jit(solution)/shard_map/ppermute | solution.py:521
  10.1 0.0 collective-permute-done.1.right.right_z
  10.1 0.0 copy-start.7
  10.1 0.0 copy-start.6
  10.1 0.0 copy-done.1
  10.1 0.7 %copy-done.7 = s32[1,2,32]{2,1,0:T(2,128)S(1)} copy-done((s32[1,2,32]{2,1,0:T(2,128)S(1)}, s32[1,2,32]{2,1,0:T(2,128)}, u32[]{:S(2)}) %copy-start.7) | copy-done | bytes 280
  10.8 0.0 copy-done.6
  10.8 0.4 %shard_map.74 = (f32[9,16,128]{2,1,0:T(8,128)S(1)}, f32[88,128]{1,0:T(8,128)S(1)}, f32[88,128]{1,0:T(8,128)S(1)}) custom-call(f32[5,16,128]{2,1,0:T(8,128)S(1)} %bitcast.12, f32[9,16,128]{2,1,0:T(8,128)S(1)} %bitcast.9, s32[2,32]{1,0:T(2,128)S(1)} %bitcast.20, s32[2,32]{1,0:T(2,128)S(1)} %bitcast.22, s32[2,32]{1,0:T(2,128)S(1)} %bitcast.17, ...), custom_call_target="tpu_custom_call" | custom-call | tf_op jit(solution)/shard_map/pallas_call | solution.py:510
  11.2 2.8 %collective-permute-start.2 = (f32[88,128]{1,0:T(8,128)S(1)}, f32[88,128]{1,0:T(8,128)S(1)}, u32[]{:S(2)}, u32[]{:S(2)}) collective-permute-start(f32[88,128]{1,0:T(8,128)S(1)} %get-tuple-element.17), channel_id=1, source_target_pairs={{0,8},{8,16},{16,24},{24,0},{1,9},{9,17},{17,25},{25,1},{2,10},{10... | collective-permute-start | bytes 135176 | tf_op jit(solution)/shard_map/ppermute | solution.py:521
  14.0 0.0 collective-permute-start.3
  14.0 1.1 %collective-permute-done.2.left_x = f32[88,128]{1,0:T(8,128)S(1)} collective-permute-done((f32[88,128]{1,0:T(8,128)S(1)}, f32[88,128]{1,0:T(8,128)S(1)}, u32[]{:S(2)}, u32[]{:S(2)}) %collective-permute-start.2) | collective-permute-done | bytes 45088 | tf_op jit(solution)/shard_map/ppermute | solution.py:521
  15.1 2.3 %collective-permute-done.3.right_x = f32[88,128]{1,0:T(8,128)S(1)} collective-permute-done((f32[88,128]{1,0:T(8,128)S(1)}, f32[88,128]{1,0:T(8,128)S(1)}, u32[]{:S(2)}, u32[]{:S(2)}) %collective-permute-start.3) | collective-permute-done | bytes 45088 | tf_op jit(solution)/shard_map/ppermute | solution.py:522
  17.4 1.0 %shard_map.75 = f32[5,16,128]{2,1,0:T(8,128)} custom-call(f32[5,16,128]{2,1,0:T(8,128)S(1)} %bitcast.13, f32[16,128]{1,0:T(8,128)S(1)} %bitcast.15, f32[9,16,128]{2,1,0:T(8,128)S(1)} %bitcast.10, s32[2,32]{1,0:T(2,128)S(1)} %bitcast.19, s32[2,32]{1,0:T(2,128)S(1)} %bitcast.21, s32[2,32]{1,0:T(2,128)S(1)} %bitcast.23, ...), custom_call_target="tpu_custom_call" | custom-call | tf_op jit(solution)/shard_map/pallas_call | solution.py:510
Async XLA Ops:
  0.0 0.7 %copy-start.3 = (f32[4,4,128]{2,1,0:T(4,128)S(1)}, f32[4,4,128]{2,1,0:T(4,128)}, u32[]{:S(2)}) copy-start(f32[4,4,128]{2,1,0:T(4,128)} %param.8) | copy-start | bytes 24580
  0.0 0.7 %copy-start.4 = (s32[2,1,32]{2,1,0:T(1,128)S(1)}, s32[2,1,32]{2,1,0:T(1,128)}, u32[]{:S(2)}) copy-start(s32[2,1,32]{2,1,0:T(1,128)} %param.11) | copy-start | bytes 772
  0.7 0.9 %copy-start = (f32[3,3,4,4,128]{4,3,2,1,0:T(4,128)S(1)}, f32[3,3,4,4,128]{4,3,2,1,0:T(4,128)}, u32[]{:S(2)}) copy-start(f32[3,3,4,4,128]{4,3,2,1,0:T(4,128)} %param.9) | copy-start | bytes 221188
  1.6 0.8 %copy-start.2 = (f32[5,4,4,128]{3,2,1,0:T(4,128)S(1)}, f32[5,4,4,128]{3,2,1,0:T(4,128)}, u32[]{:S(2)}) copy-start(f32[5,4,4,128]{3,2,1,0:T(4,128)} %param.7) | copy-start | bytes 122884
  2.4 0.7 %copy-start.5 = (s32[2,1,32]{2,1,0:T(1,128)S(1)}, s32[2,1,32]{2,1,0:T(1,128)}, u32[]{:S(2)}) copy-start(s32[2,1,32]{2,1,0:T(1,128)} %param.10) | copy-start | bytes 772
  3.0 7.0 %copy-start.1 = (f32[3,3,4,4,128]{4,3,2,1,0:T(4,128)S(1)}, f32[3,3,4,4,128]{4,3,2,1,0:T(4,128)}, u32[]{:S(2)}) copy-start(f32[3,3,4,4,128]{4,3,2,1,0:T(4,128)} %param.9) | copy-start | bytes 221188
  3.3 6.7 %collective-permute-start = (f32[96,128]{1,0:T(8,128)S(1)}, f32[96,128]{1,0:T(8,128)S(1)}, u32[]{:S(2)}, u32[]{:S(2)}) collective-permute-start(f32[96,128]{1,0:T(8,128)S(1)} %get-tuple-element.14), channel_id=1, source_target_pairs={{0,1},{1,2},{2,3},{3,4},{4,5},{5,6},{6,7},{7,0},{8,9},{9,10},{10,1... | collective-permute-start | bytes 147464 | tf_op jit(solution)/shard_map/ppermute | solution.py:521
  5.5 4.6 %collective-permute-start.1 = (f32[96,128]{1,0:T(8,128)S(1)}, f32[96,128]{1,0:T(8,128)S(1)}, u32[]{:S(2)}, u32[]{:S(2)}) collective-permute-start(f32[96,128]{1,0:T(8,128)S(1)} %get-tuple-element.15), channel_id=1, source_target_pairs={{1,0},{2,1},{3,2},{4,3},{5,4},{6,5},{7,6},{0,7},{9,8},{10,9},{11,1... | collective-permute-start | bytes 147464 | tf_op jit(solution)/shard_map/ppermute | solution.py:522
  10.1 0.7 %copy-start.7 = (s32[1,2,32]{2,1,0:T(2,128)S(1)}, s32[1,2,32]{2,1,0:T(2,128)}, u32[]{:S(2)}) copy-start(s32[1,2,32]{2,1,0:T(2,128)} %param.13) | copy-start | bytes 772
  10.1 0.7 %copy-start.6 = (s32[1,2,32]{2,1,0:T(2,128)S(1)}, s32[1,2,32]{2,1,0:T(2,128)}, u32[]{:S(2)}) copy-start(s32[1,2,32]{2,1,0:T(2,128)} %param.12) | copy-start | bytes 772
  11.2 3.9 %collective-permute-start.2 = (f32[88,128]{1,0:T(8,128)S(1)}, f32[88,128]{1,0:T(8,128)S(1)}, u32[]{:S(2)}, u32[]{:S(2)}) collective-permute-start(f32[88,128]{1,0:T(8,128)S(1)} %get-tuple-element.17), channel_id=1, source_target_pairs={{0,8},{8,16},{16,24},{24,0},{1,9},{9,17},{17,25},{25,1},{2,10},{10... | collective-permute-start | bytes 135176 | tf_op jit(solution)/shard_map/ppermute | solution.py:521
  14.0 3.5 %collective-permute-start.3 = (f32[88,128]{1,0:T(8,128)S(1)}, f32[88,128]{1,0:T(8,128)S(1)}, u32[]{:S(2)}, u32[]{:S(2)}) collective-permute-start(f32[88,128]{1,0:T(8,128)S(1)} %get-tuple-element.18), channel_id=1, source_target_pairs={{8,0},{16,8},{24,16},{0,24},{9,1},{17,9},{25,17},{1,25},{10,2},{18... | collective-permute-start | bytes 135176 | tf_op jit(solution)/shard_map/ppermute | solution.py:522
where the time goes:
time: 18.7 us; the launch traced here: 18.4 us
  starting transfers between devices  7.97 us (43%)
  waiting for transfers between devices  4.99 us (27%)
  local copies, waits for them, and re-layouts  3.73 us (20%)
  Pallas kernels  1.72 us (9%)
    ppermute x2, starting transfers between devices, exchange(): lax.ppermute(up, axis, [(i, (i + 1) % count) for i in range(count)])  4.86 us
    unnamed x16, local copies, waits for them, and re-layouts  3.73 us
    ppermute x2, starting transfers between devices, exchange(): lax.ppermute(low, axis, [((i + 1) % count, i) for i in range(count)])  3.11 us
    ppermute x2, waiting for transfers between devices, exchange(): lax.ppermute(up, axis, [(i, (i + 1) % count) for i in range(count)])  2.65 us
    ppermute x2, waiting for transfers between devices, exchange(): lax.ppermute(low, axis, [((i + 1) % count, i) for i in range(count)])  2.33 us
    pallas_call x3, Pallas kernels, call(): pl.pallas_call(kernel, out_shape=[jax.ShapeDtypeStruct(s, jnp.float32) fo...  1.72 us
  transfers between devices with their start and end apart: 4, of which 3 were waited for; matrix products, arithmetic and copies ran while one was open for 0% of the time, Pallas kernels for 0%

commit v1 on v0

--- a/solution.py
+++ b/solution.py
@@ -165,9 +165,17 @@
     ]
 
 
-def normal_flux(state, velocity, pressure, slopes, normal):
+def plain_flux(state, velocity, pressure, normal):
+    speed = velocity[0] * normal[0] + velocity[1] * normal[1] + velocity[2] * normal[2]
+    out = [state[0] * speed]
+    for j in range(3):
+        out.append(state[1 + j] * speed + pressure * normal[j])
+    out.append((state[4] + pressure) * speed)
+    return out, speed
+
+
+def drag_flux(velocity, slopes, normal):
     m0, m1, m2 = normal
-    speed = velocity[0] * m0 + velocity[1] * m1 + velocity[2] * m2
     spread = (visc_coef * 2.0 / 3.0) * (slopes[0] + slopes[1] + slopes[2])
     t00, t11, t22 = [2.0 * visc_coef * slopes[d] - spread for d in range(3)]
     t01, t02, t12 = [visc_coef * slopes[3 + d] for d in range(3)]
@@ -178,11 +186,7 @@
     ]
     heat = heat_coef * (slopes[6] * m0 + slopes[7] * m1 + slopes[8] * m2)
     work = velocity[0] * stress[0] + velocity[1] * stress[1] + velocity[2] * stress[2]
-    out = [state[0] * speed]
-    for j in range(3):
-        out.append(state[1 + j] * speed + pressure * normal[j] - stress[j])
-    out.append((state[4] + pressure) * speed - work - heat)
-    return out, speed, heat
+    return stress + [work + heat], heat
 
 
 def wave(speed, theta, normal_size):
@@ -279,9 +283,31 @@
     return [jnp.where(take_before, pltpu.roll(r, 1, 1), r) for r in rows]
 
 
-def first_kernel(cons, jac, met, xm_ref, xf_ref, grad_out, turned_out, low_out, up_out):
+def first_kernel(
+    cons_in, jac_in, met_in, xm_in, xf_in, zm_in, zf_in,
+    cons, jac, met, zm_out, zf_out, index_out, grad_out, turned_out, low_out, up_out,
+    xm_ref, xf_ref, sems,
+):
+    copies = [
+        pltpu.make_async_copy(a, b, sems.at[i])
+        for i, (a, b) in enumerate(
+            [
+                (met_in, met),
+                (cons_in, cons),
+                (jac_in, jac),
+                (xf_in, xf_ref),
+                (xm_in, xm_ref),
+                (zf_in, zf_out),
+                (zm_in, zm_out),
+            ]
+        )
+    ]
+    for c in copies:
+        c.start()
     frame = Frame(cons.shape[-1])
     frame.deriv_weights()
+    for c in copies[::-1]:
+        c.wait()
     state = load_state(cons)
     rows = [load_rows(met, g) for g in range(3)]
     lifted = []
@@ -316,8 +342,12 @@
     inverse = [1.0 / jac[0:8, :], 1.0 / jac[8:16, :]]
     state_f = by_field(state)
     code = spread_flags(frame, xf_ref[...])
-    lead = spread_flags(frame, xm_ref[...]) == 1
+    master = spread_flags(frame, xm_ref[...])
+    lead = master == 1
     indices = turn_indices(frame, code, True)
+    for k in range(3):
+        index_out[8 * k : 8 * k + 8, :] = indices[k]
+    index_out[24:32, :] = master
     own_x = [frame.face_x(p) for p in state_f + by_field(rows[0])]
     turned = [turn(p, indices) for p in own_x + [frame.face_x(inverse)]]
     for f in range(9):
@@ -337,32 +367,80 @@
     pack(frame, faces + edges, low_out, up_out)
 
 
+def first_cover(cons, met, zm_ref, zf_ref, index_out, part_out):
+    frame = Frame(cons.shape[-1])
+    frame.deriv_weights()
+    indices = turn_indices(frame, spread_flags(frame, zf_ref[...]), False)
+    for k in range(3):
+        index_out[8 * k : 8 * k + 8, :] = indices[k]
+    index_out[24:32, :] = spread_flags(frame, zm_ref[...])
+    state = load_state(cons)
+    rows = [load_rows(met, g) for g in range(3)]
+    sign_y = frame.sign_lanes()
+    up_lane = frame.point_lane == 3
+    wall = (frame.lane == 0) | (frame.lane == frame.lanes - 1)
+    volume = []
+    lane_flux = []
+    for t in range(2):
+        velocity, pressure, theta = primitive(state[t])
+        volume.append([plain_flux(state[t], velocity, pressure, rows[g][t])[0] for g in range(3)])
+        normal = lane_normal(frame, rows[2][t])
+        half, speed = plain_flux(state[t], velocity, pressure, normal)
+        own_wave = wave(speed, theta, size_of(normal))
+        fastest = jnp.maximum(own_wave, lane_partner(frame, own_wave, False))
+        mirrored = [-half[0], half[1], half[2], half[3], -half[4]]
+        direction = jnp.where(up_lane, jnp.float32(0.5), jnp.float32(-0.5)) * fastest
+        result = []
+        for c in range(5):
+            other_half = jnp.where(wall, mirrored[c], lane_partner(frame, half[c], False))
+            other_state = lane_partner(frame, state[t][c], 1 <= c <= 3)
+            result.append(0.5 * (half[c] + other_half) - direction * (other_state - state[t][c]))
+        lane_flux.append(result)
+    for c in range(5):
+        dx = frame.deriv_x([volume[t][0][c] for t in range(2)])
+        for t in range(2):
+            part_out[c, 8 * t : 8 * t + 8, :] = (
+                dx[t]
+                + frame.deriv_rows(volume[t][1][c])
+                + frame.deriv_lanes(volume[t][2][c])
+                + sign_y * lane_flux[t][c]
+            )
+
+
+def load_indices(ref):
+    return [ref[8 * k : 8 * k + 8, :] for k in range(3)]
+
+
+def mean_of(prim1, prim2):
+    return [0.5 * (a + b) for a, b in zip(prim1[0] + [prim1[2]], prim2[0] + [prim2[2]])]
+
+
+def first_of_pair(frame):
+    return jnp.full((8, frame.lanes), lax.axis_index("gx") % 2) == 0
+
+
 def second_kernel(
-    cons, met, zm_ref, zf_ref, xf_ref, grad_in, turned_in, left, right, grad_out, low_out, up_out
+    cons, met, x_index, z_index, grad_in, turned_in, left, right, grad_out, part_out, near_out, far_out
 ):
     frame = Frame(cons.shape[-1])
-    code = spread_flags(frame, zf_ref[...])
-    lead = spread_flags(frame, zm_ref[...]) == 1
-    indices = turn_indices(frame, code, False)
+    lead = z_index[24:32, :] == 1
+    indices = load_indices(z_index)
+    x_indices = load_indices(x_index)
     got = unpack(frame, left, right, 23)
     other = [turn(p, indices) for p in got[:8]]
     own = [frame.face_z(load_pair(cons, f)) for f in range(5)]
     own_rows = [frame.face_z(load_pair(met, 3 + d)) for d in range(3)]
-    velocity, _, theta = primitive(own)
-    velocity2, _, theta2 = primitive(other[:5])
-    mean = [0.5 * (a + b) for a, b in zip(velocity + [theta], velocity2 + [theta2])]
     normal = [jnp.where(lead, own_rows[d], other[5 + d]) for d in range(3)]
-    part = combos(mean, normal)
+    part = combos(mean_of(primitive(own), primitive(other[:5])), normal)
     sign = frame.sign_rows()
     faces = []
-    x_code = spread_flags(frame, xf_ref[...])
-    x_indices = turn_indices(frame, x_code, True)
     for f in range(9):
         spread = frame.spread_z(part[f])
         total = [grad_in[f, 8 * t : 8 * t + 8, :] + sign * spread[t] for t in range(2)]
         for t in range(2):
             grad_out[f, 8 * t : 8 * t + 8, :] = total[t]
         faces.append(turn(frame.face_x(total), x_indices))
+        part_out[8 * f : 8 * f + 8, :] = part[f]
     turned = [turned_in[8 * f : 8 * f + 8, :] for f in range(9)]
     odd = frame.point_row % 2
     high = jnp.where(frame.point_row >= 2, 4, 0)
@@ -371,11 +449,50 @@
     lines = [sub_gather(got[18], both), sub_gather(got[19], both)]
     lines.append(jnp.where(odd == 0, sub_gather(got[20], outer), sub_gather(got[21], outer)))
     lines.append(sub_gather(got[22], outer))
-    pack(frame, turned + faces + lines, low_out, up_out)
+    lower = first_of_pair(frame)
+    fields = turned + faces + lines
+    for g in range(len(fields) // 2):
+        a, b = fields[2 * g], fields[2 * g + 1]
+        low = jnp.where(frame.low_half, a, frame.swap(b))
+        up = jnp.where(frame.low_half, frame.swap(a), b)
+        near_out[8 * g : 8 * g + 8, :] = jnp.where(lower, up, low)
+        far_out[8 * g : 8 * g + 8, :] = jnp.where(lower, low, up)
+
+
+def plain_face(own, own_prim, other, other_prim, normal, side_sign):
+    size = size_of(normal)
+    flux1, speed1 = plain_flux(own, own_prim[0], own_prim[1], normal)
+    flux2, speed2 = plain_flux(other, other_prim[0], other_prim[1], normal)
+    fastest = jnp.maximum(wave(speed1, own_prim[2], size), wave(speed2, other_prim[2], size))
+    half = 0.5 * side_sign * fastest
+    return [0.5 * (flux1[c] + flux2[c]) - half * (other[c] - own[c]) for c in range(5)]
+
+
+def second_cover(cons, met, z_index, part_in, left, right, part_out, face_out):
+    frame = Frame(cons.shape[-1])
+    lead = z_index[24:32, :] == 1
+    indices = load_indices(z_index)
+    got = unpack(frame, left, right, 9)
+    turned = [turn(p, indices) for p in got]
+    other = turned[:5]
+    other_prim = primitive(other)
+    own = [frame.face_z(load_pair(cons, f)) for f in range(5)]
+    own_rows = [frame.face_z(load_pair(met, 3 + d)) for d in range(3)]
+    own_prim = primitive(own)
+    normal = [jnp.where(lead, own_rows[d], turned[5 + d]) for d in range(3)]
+    flux = plain_face(own, own_prim, other, other_prim, normal, frame.sides(-1.0, 1.0))
+    sign = frame.sign_rows()
+    for c in range(5):
+        spread = frame.spread_z(flux[c])
+        for t in range(2):
+            part_out[c, 8 * t : 8 * t + 8, :] = part_in[c, 8 * t : 8 * t + 8, :] + sign * spread[t]
+    for i, tile in enumerate(own_prim[0] + other_prim[0] + normal + [turned[8]]):
+        face_out[8 * i : 8 * i + 8, :] = tile
 
 
 def third_kernel(
-    cons, jac, met, xm_ref, zm_ref, zf_ref, grad_in, left_z, right_z, left_x, right_x, out
+    cons, jac, met, x_index, z_index, grad_in, lift_in, part_in, face_in,
+    left_z, right_z, near_x, far_x, out,
 ):
     frame = Frame(cons.shape[-1])
     frame.deriv_weights()
@@ -383,14 +500,19 @@
     state_f = by_field(state)
     rows = [load_rows(met, g) for g in range(3)]
     inverse = [1.0 / jac[0:8, :], 1.0 / jac[8:16, :]]
-    prims = [primitive(state[t]) for t in range(2)]
     got_z = unpack(frame, left_z, right_z, 23)
-    got_x = unpack(frame, left_x, right_x, 22)
-    x_lead = spread_flags(frame, xm_ref[...]) == 1
-    z_lead = spread_flags(frame, zm_ref[...]) == 1
-    z_indices = turn_indices(frame, spread_flags(frame, zf_ref[...]), False)
+    lower = first_of_pair(frame)
+    got_x = []
+    for g in range(11):
+        near = near_x[8 * g : 8 * g + 8, :]
+        far = far_x[8 * g : 8 * g + 8, :]
+        left = jnp.where(lower, far, near)
+        right = jnp.where(lower, near, far)
+        got_x.append(jnp.where(frame.low_half, left, frame.swap(right)))
+        got_x.append(jnp.where(frame.low_half, frame.swap(left), right))
+    x_lead = x_index[24:32, :] == 1
+    z_indices = load_indices(z_index)
     face_sign = frame.sides(-lift, lift)
-    side_sign = frame.sides(-1.0, 1.0)
 
     own = [frame.face_x(p) for p in state_f]
     own_rows = [frame.face_x(p) for p in by_field(rows[0])]
@@ -398,11 +520,7 @@
     other = got_x[:5]
     other_prim = primitive(other)
     normal_x = [jnp.where(x_lead, own_rows[d], got_x[5 + d]) for d in range(3)]
-    mean = [
-        0.5 * (a + b)
-        for a, b in zip(own_prim[0] + [own_prim[2]], other_prim[0] + [other_prim[2]])
-    ]
-    part = combos(mean, normal_x)
+    part = combos(mean_of(own_prim, other_prim), normal_x)
     slopes = []
     for f in range(9):
         lifted_part = face_sign * part[f]
@@ -414,18 +532,10 @@
         slopes.append([tiles[t] * inverse[t] for t in range(2)])
     own_slopes = [frame.face_x(p) for p in slopes]
     other_slopes = [(got_x[9 + f] - face_sign * part[f]) * got_x[8] for f in range(9)]
-
-    def face_flux(own, own_prim, own_slopes, other, other_prim, other_slopes, normal):
-        size = size_of(normal)
-        flux1, speed1, _ = normal_flux(own, own_prim[0], own_prim[1], own_slopes, normal)
-        flux2, speed2, _ = normal_flux(other, other_prim[0], other_prim[1], other_slopes, normal)
-        fastest = jnp.maximum(wave(speed1, own_prim[2], size), wave(speed2, other_prim[2], size))
-        half = 0.5 * side_sign * fastest
-        return [
-            0.5 * (flux1[c] + flux2[c]) - half * (other[c] - own[c]) for c in range(5)
-        ]
-
-    flux_x = face_flux(own, own_prim, own_slopes, other, other_prim, other_slopes, normal_x)
+    flux_x = plain_face(own, own_prim, other, other_prim, normal_x, frame.sides(-1.0, 1.0))
+    drag1 = drag_flux(own_prim[0], own_slopes, normal_x)[0]
+    drag2 = drag_flux(other_prim[0], other_slopes, normal_x)[0]
+    flux_x = [flux_x[0]] + [flux_x[1 + c] - 0.5 * (drag1[c] + drag2[c]) for c in range(4)]
 
     edge_a = jnp.where(frame.low_half, 0, 2) + jnp.where(frame.point_row >= 2, 4, 0)
     edge_b = edge_a + 1
@@ -447,72 +557,67 @@
     edge_part = combos(edge_mean, line_rows)
     edge_sign = frame.sign_rows()
     other_grad = [turn(got_z[9 + f] + edge_sign * edge_part[f], z_indices) for f in range(9)]
-    turned = [turn(p, z_indices) for p in got_z[:9]]
-    other = turned[:5]
-    other_prim = primitive(other)
-    own = [frame.face_z(p) for p in state_f]
-    own_prim = primitive(own)
-    own_rows = [frame.face_z(p) for p in by_field(rows[1])]
-    normal_z = [jnp.where(z_lead, own_rows[d], turned[5 + d]) for d in range(3)]
-    mean = [
-        0.5 * (a + b)
-        for a, b in zip(own_prim[0] + [own_prim[2]], other_prim[0] + [other_prim[2]])
+    face = [face_in[8 * i : 8 * i + 8, :] for i in range(10)]
+    normal_z = face[6:9]
+    other_slopes = [
+        (other_grad[f] - face_sign * lift_in[8 * f : 8 * f + 8, :]) * face[9] for f in range(9)
     ]
-    part = combos(mean, normal_z)
-    other_slopes = [(other_grad[f] - face_sign * part[f]) * turned[8] for f in range(9)]
     own_slopes = [frame.face_z(p) for p in slopes]
-    flux_z = face_flux(own, own_prim, own_slopes, other, other_prim, other_slopes, normal_z)
+    drag1 = drag_flux(face[0:3], own_slopes, normal_z)[0]
+    drag2 = drag_flux(face[3:6], other_slopes, normal_z)[0]
+    drag_z = [0.5 * (drag1[c] + drag2[c]) for c in range(4)]
 
     slopes_t = [[slopes[f][t] for f in range(9)] for t in range(2)]
     sign_y = frame.sign_lanes()
-    up_lane = frame.point_lane == 3
     wall = (frame.lane == 0) | (frame.lane == frame.lanes - 1)
     volume = []
     lane_flux = []
     for t in range(2):
-        velocity, pressure, theta = prims[t]
-        volume.append(
-            [normal_flux(state[t], velocity, pressure, slopes_t[t], rows[g][t])[0] for g in range(3)]
-        )
+        velocity = primitive(state[t])[0]
+        volume.append([drag_flux(velocity, slopes_t[t], rows[g][t])[0] for g in range(3)])
         normal = lane_normal(frame, rows[2][t])
-        half, speed, heat = normal_flux(state[t], velocity, pressure, slopes_t[t], normal)
-        own_wave = wave(speed, theta, size_of(normal))
-        fastest = jnp.maximum(own_wave, lane_partner(frame, own_wave, False))
-        mirrored = [-half[0], half[1], half[2], half[3], -half[4] - 2.0 * heat]
-        direction = jnp.where(up_lane, jnp.float32(0.5), jnp.float32(-0.5)) * fastest
+        half, heat = drag_flux(velocity, slopes_t[t], normal)
+        mirrored = [half[0], half[1], half[2], 2.0 * heat - half[3]]
         result = []
-        for c in range(5):
+        for c in range(4):
             other_half = jnp.where(wall, mirrored[c], lane_partner(frame, half[c], False))
-            other_state = lane_partner(frame, state[t][c], 1 <= c <= 3)
-            result.append(
-                0.5 * (half[c] + other_half) - direction * (other_state - state[t][c])
-            )
+            result.append(0.5 * (half[c] + other_half))
         lane_flux.append(result)
     row_sign = frame.sign_rows()
     for c in range(5):
-        dx = frame.deriv_x([volume[t][0][c] for t in range(2)])
-        spread = frame.spread_z(flux_z[c])
         side = face_sign * flux_x[c]
         zero = jnp.zeros_like(side)
+        sides = [jnp.where(frame.low_half, side, zero), jnp.where(frame.low_half, zero, side)]
+        totals = [part_in[c, 8 * t : 8 * t + 8, :] + sides[t] for t in range(2)]
+        if c > 0:
+            k = c - 1
+            dx = frame.deriv_x([volume[t][0][k] for t in range(2)])
+            spread = frame.spread_z(drag_z[k])
+            for t in range(2):
+                totals[t] = totals[t] - (
+                    dx[t]
+                    + frame.deriv_rows(volume[t][1][k])
+                    + frame.deriv_lanes(volume[t][2][k])
+                    + sign_y * lane_flux[t][k]
+                    + row_sign * spread[t]
+                )
         for t in range(2):
-            total = (
-                dx[t]
-                + frame.deriv_rows(volume[t][1][c])
-                + frame.deriv_lanes(volume[t][2][c])
-                + sign_y * lane_flux[t][c]
-                + row_sign * spread[t]
-                + (jnp.where(frame.low_half, side, zero) if t == 0 else jnp.where(frame.low_half, zero, side))
-            )
-            out[c, 8 * t : 8 * t + 8, :] = -total * inverse[t]
-
-
-def call(kernel, outs, *args):
+            out[c, 8 * t : 8 * t + 8, :] = -totals[t] * inverse[t]
+
+
+def shaped(*shape, dtype=jnp.float32):
+    return jax.ShapeDtypeStruct(shape, dtype)
+
+
+def call(kernel, outs, *args, in_specs=None, scratch=(), flops=0):
     return pl.pallas_call(
         kernel,
-        out_shape=[jax.ShapeDtypeStruct(s, jnp.float32) for s in outs],
-        in_specs=[whole] * len(args),
+        out_shape=outs,
+        in_specs=in_specs or [whole] * len(args),
         out_specs=[whole] * len(outs),
+        scratch_shapes=scratch,
         compiler_params=pltpu.CompilerParams(vmem_limit_bytes=vmem_bytes),
+        cost_estimate=pl.CostEstimate(flops=flops, bytes_accessed=200_000, transcendentals=0),
     )(*args)
 
 
@@ -521,6 +626,18 @@
     from_left = lax.ppermute(up, axis, [(i, (i + 1) % count) for i in range(count)])
     from_right = lax.ppermute(low, axis, [((i + 1) % count, i) for i in range(count)])
     return from_left, from_right
+
+
+def exchange_pairs(near, far, axis):
+    count = lax.axis_size(axis)
+    assert count % 2 == 0
+    swaps = [[], []]
+    for k in range(count):
+        a, b = k, (k + 1) % count
+        swaps[k % 2] += [(a, b), (b, a)]
+    got_far = lax.ppermute(far, axis, swaps[1])
+    got_near = lax.ppermute(near, axis, swaps[0])
+    return got_near, got_far
 
 
 def local(conserved, jacobian, metric, x_master, x_flip, z_master, z_flip):
@@ -531,22 +648,55 @@
     jac = jacobian.reshape(nodes, lanes)
     met = metric.reshape(9, nodes, lanes)
     xm, xf, zm, zf = [a.reshape(2, a.shape[-1]) for a in (x_master, x_flip, z_master, z_flip)]
-    grad, turned, low_z, up_z = call(
+    flag = (2, xm.shape[-1])
+    cons, jac, met, zm, zf, x_index, grad, turned, low_z, up_z = call(
         first_kernel,
-        [(9, nodes, lanes), (72, lanes), (96, lanes), (96, lanes)],
-        cons, jac, met, xm, xf,
+        [
+            shaped(5, nodes, lanes),
+            shaped(nodes, lanes),
+            shaped(9, nodes, lanes),
+            shaped(*flag, dtype=jnp.int32),
+            shaped(*flag, dtype=jnp.int32),
+            shaped(32, lanes, dtype=jnp.int32),
+            shaped(9, nodes, lanes),
+            shaped(72, lanes),
+            shaped(96, lanes),
+            shaped(96, lanes),
+        ],
+        *[pltpu.with_memory_space_constraint(a, pltpu.HBM) for a in (cons, jac, met, xm, xf, zm, zf)],
+        in_specs=[pl.BlockSpec(memory_space=pltpu.HBM)] * 7,
+        scratch=[
+            pltpu.VMEM(flag, jnp.int32),
+            pltpu.VMEM(flag, jnp.int32),
+            pltpu.SemaphoreType.DMA((7,)),
+        ],
+        flops=1_000_000,
     )
     left_z, right_z = exchange(low_z, up_z, "gz")
-    grad, low_x, up_x = call(
+    z_index, part = call(
+        first_cover,
+        [shaped(32, lanes, dtype=jnp.int32), shaped(5, nodes, lanes)],
+        cons, met, zm, zf,
+        flops=1_000_000,
+    )
+    grad, lift_z, near_x, far_x = call(
         second_kernel,
-        [(9, nodes, lanes), (88, lanes), (88, lanes)],
-        cons, met, zm, zf, xf, grad, turned, left_z, right_z,
-    )
-    left_x, right_x = exchange(low_x, up_x, "gx")
+        [shaped(9, nodes, lanes), shaped(72, lanes), shaped(88, lanes), shaped(88, lanes)],
+        cons, met, x_index, z_index, grad, turned, left_z, right_z,
+        flops=1_000_000,
+    )
+    near_x, far_x = exchange_pairs(near_x, far_x, "gx")
+    part, face = call(
+        second_cover,
+        [shaped(5, nodes, lanes), shaped(80, lanes)],
+        cons, met, z_index, part, left_z, right_z,
+        flops=1_000_000,
+    )
     (rhs,) = call(
         third_kernel,
-        [(5, nodes, lanes)],
-        cons, jac, met, xm, zm, zf, grad, left_z, right_z, left_x, right_x,
+        [shaped(5, nodes, lanes)],
+        cons, jac, met, x_index, z_index, grad, lift_z, part, face, left_z, right_z, near_x, far_x,
+        flops=1_000_000,
     )
     return rhs.reshape(conserved.shape)
 

time: 18.7 us -> 14.4 us (0.77)
  local copies, waits for them, and re-layouts: 3.73 us -> 0 us
  waiting for transfers between devices: 4.99 us -> 3.28 us
  Pallas kernels: 1.72 us -> 2.81 us
    unnamed x16 -> x0, local copies, waits for them, and re-layouts: 3.73 us -> none
    ppermute x0 -> x2, starting transfers between devices: none -> 2.84 us  [the longest x1 1.54 us: exchange_pairs(): got_near = lax.ppermute(near, axis, swaps[0])]
    ppermute x2 -> x1, starting transfers between devices: 4.86 us -> 2.11 us  [exchange(): lax.ppermute(up, axis, [(i, (i + 1) % count) for i in range(count)])]
    ppermute x2 -> x1, waiting for transfers between devices: 2.33 us -> 0.01 us  [exchange(): lax.ppermute(low, axis, [((i + 1) % count, i) for i in range(count)])]
    ppermute x0 -> x2, waiting for transfers between devices: none -> 1.98 us  [the longest x1 1.98 us: exchange_pairs(): got_far = lax.ppermute(far, axis, swaps[1])]
    ppermute x2 -> x1, waiting for transfers between devices: 2.65 us -> 1.29 us  [exchange(): lax.ppermute(up, axis, [(i, (i + 1) % count) for i in range(count)])]
    pallas_call x3 -> x5, Pallas kernels: 1.72 us -> 2.81 us  [call(): pl.pallas_call(kernel, out_shape=outs, in_specs=in_specs or [whole] * len...]
    ppermute x2 -> x1, starting transfers between devices: 3.11 us -> 3.1 us  [exchange(): lax.ppermute(low, axis, [((i + 1) % count, i) for i in range(count)])]
  transfers between devices with their start and end apart: 4 -> 4, of which waited for: 3 -> 2; matrix products, arithmetic and copies ran while one was open for 0% -> 0% of each run, Pallas kernels for 0% -> 3%
where the time goes in v1:
time: 14.4 us; the launch traced here: 14.2 us
  starting transfers between devices  8.06 us (56%)
  waiting for transfers between devices  3.28 us (23%)
  Pallas kernels  2.81 us (20%)
    ppermute x1, starting transfers between devices, exchange(): lax.ppermute(low, axis, [((i + 1) % count, i) for i in range(count)])  3.1 us
    pallas_call x5, Pallas kernels, call(): pl.pallas_call(kernel, out_shape=outs, in_specs=in_specs or [whole] * len...  2.81 us
    ppermute x1, starting transfers between devices, exchange(): lax.ppermute(up, axis, [(i, (i + 1) % count) for i in range(count)])  2.11 us
    ppermute x1, waiting for transfers between devices, exchange_pairs(): got_far = lax.ppermute(far, axis, swaps[1])  1.98 us
    ppermute x1, starting transfers between devices, exchange_pairs(): got_near = lax.ppermute(near, axis, swaps[0])  1.54 us
    ppermute x1, starting transfers between devices, exchange_pairs(): got_far = lax.ppermute(far, axis, swaps[1])  1.3 us
    ppermute x1, waiting for transfers between devices, exchange(): lax.ppermute(up, axis, [(i, (i + 1) % count) for i in range(count)])  1.29 us
  transfers between devices with their start and end apart: 4, of which 2 were waited for; matrix products, arithmetic and copies ran while one was open for 0% of the time, Pallas kernels for 3%

profile of v1, /device:TPU:1, one launch (start us, length us, event | category | flops | bytes accessed | tf_op | source)
XLA Modules:
  0.0 14.2 jit_solution(14650588551848915156)
XLA Ops:
  0.0 1.2 %shard_map.73 = (f32[5,16,128]{2,1,0:T(8,128)S(1)}, f32[16,128]{1,0:T(8,128)S(1)}, f32[9,16,128]{2,1,0:T(8,128)S(1)}, s32[2,32]{1,0:T(2,128)S(1)}, s32[2,32]{1,0...) custom-call(f32[5,16,128]{2,1,0:T(8,128)} %bitcast.9, ...), custom_call_target="tpu_custom_call" | custom-call | flops 1000000 | bytes 200000 | tf_op jit(solution)/shard_map/pallas_call | solution.py:613
  1.2 2.1 %collective-permute-start = (f32[96,128]{1,0:T(8,128)S(1)}, f32[96,128]{1,0:T(8,128)S(1)}, u32[]{:S(2)}, u32[]{:S(2)}) collective-permute-start(f32[96,128]{1,0:T(8,128)S(1)} %get-tuple-element.32), channel_id=1, source_target_pairs={{0,1},{1,2},{2,3},{3,4},{4,5},{5,6},{6,7},{7,0},{8,9},{9,10},{10,1... | collective-permute-start | bytes 147464 | tf_op jit(solution)/shard_map/ppermute | solution.py:626
  3.4 3.1 %collective-permute-start.1 = (f32[96,128]{1,0:T(8,128)S(1)}, f32[96,128]{1,0:T(8,128)S(1)}, u32[]{:S(2)}, u32[]{:S(2)}) collective-permute-start(f32[96,128]{1,0:T(8,128)S(1)} %get-tuple-element.33), channel_id=1, source_target_pairs={{1,0},{2,1},{3,2},{4,3},{5,4},{6,5},{7,6},{0,7},{9,8},{10,9},{11,1... | collective-permute-start | bytes 147464 | tf_op jit(solution)/shard_map/ppermute | solution.py:627
  6.5 0.2 %shard_map.74 = (s32[32,128]{1,0:T(8,128)S(1)}, f32[5,16,128]{2,1,0:T(8,128)S(1)}) custom-call(f32[5,16,128]{2,1,0:T(8,128)S(1)} %get-tuple-element.23.cons, f32[9,16,128]{2,1,0:T(8,128)S(1)} %get-tuple-element.25.met, s32[2,32]{1,0:T(2,128)S(1)} %get-tuple-element.27.zm_ref, s32[2,32]{1,0:T(2,128)S(1)} %get-tuple-element.28.zf_ref), custom_call_target="tpu_custom_call" | custom-call | flops 1000000 | bytes 200000 | tf_op jit(solution)/shard_map/pallas_call | solution.py:613
  6.7 1.3 %collective-permute-done.left.left_z = f32[96,128]{1,0:T(8,128)S(1)} collective-permute-done((f32[96,128]{1,0:T(8,128)S(1)}, f32[96,128]{1,0:T(8,128)S(1)}, u32[]{:S(2)}, u32[]{:S(2)}) %collective-permute-start) | collective-permute-done | bytes 49184 | tf_op jit(solution)/shard_map/ppermute | solution.py:626
  8.0 0.0 collective-permute-done.1.right.right_z
  8.0 0.3 %shard_map.75 = (f32[9,16,128]{2,1,0:T(8,128)S(1)}, f32[72,128]{1,0:T(8,128)S(1)}, f32[88,128]{1,0:T(8,128)S(1)}, f32[88,128]{1,0:T(8,128)S(1)}) custom-call(f32[5,16,128]{2,1,0:T(8,128)S(1)} %get-tuple-element.23.cons, f32[9,16,128]{2,1,0:T(8,128)S(1)} %get-tuple-element.25.met, s32[32,128]{1,0:T(8,128)S(1)} %get-tuple-element.26.x_index, ...), custom_call_target="tpu_custom_call" | custom-call | flops 1000000 | bytes 200000 | tf_op jit(solution)/shard_map/pallas_call | solution.py:613
  8.3 1.5 %collective-permute-start.2 = (f32[88,128]{1,0:T(8,128)S(1)}, f32[88,128]{1,0:T(8,128)S(1)}, u32[]{:S(2)}, u32[]{:S(2)}) collective-permute-start(f32[88,128]{1,0:T(8,128)S(1)} %get-tuple-element.39), channel_id=1, source_target_pairs={{0,8},{8,0},{16,24},{24,16},{1,9},{9,1},{17,25},{25,17},{2,10},{10... | collective-permute-start | bytes 135176 | tf_op jit(solution)/shard_map/ppermute | solution.py:639
  9.8 1.3 %collective-permute-start.3 = (f32[88,128]{1,0:T(8,128)S(1)}, f32[88,128]{1,0:T(8,128)S(1)}, u32[]{:S(2)}, u32[]{:S(2)}) collective-permute-start(f32[88,128]{1,0:T(8,128)S(1)} %get-tuple-element.40), channel_id=1, source_target_pairs={{8,16},{16,8},{24,0},{0,24},{9,17},{17,9},{25,1},{1,25},{10,18},{1... | collective-permute-start | bytes 135176 | tf_op jit(solution)/shard_map/ppermute | solution.py:638
  11.1 0.2 %shard_map.76 = (f32[5,16,128]{2,1,0:T(8,128)S(1)}, f32[80,128]{1,0:T(8,128)S(1)}) custom-call(f32[5,16,128]{2,1,0:T(8,128)S(1)} %get-tuple-element.23.cons, f32[9,16,128]{2,1,0:T(8,128)S(1)} %get-tuple-element.25.met, s32[32,128]{1,0:T(8,128)S(1)} %get-tuple-element.29.z_index, f32[5,16,128]{2,1,0:T(8,128)S(1)} %get-tuple-element.36.part_in, ...), custom_call_target="tpu_custom_call" | custom-call | flops 1000000 | bytes 200000 | tf_op jit(solution)/shard_map/pallas_call | solution.py:613
  11.3 0.0 collective-permute-done.2.near_x
  11.3 2.0 %collective-permute-done.3.far_x = f32[88,128]{1,0:T(8,128)S(1)} collective-permute-done((f32[88,128]{1,0:T(8,128)S(1)}, f32[88,128]{1,0:T(8,128)S(1)}, u32[]{:S(2)}, u32[]{:S(2)}) %collective-permute-start.3) | collective-permute-done | bytes 45088 | tf_op jit(solution)/shard_map/ppermute | solution.py:638
  13.3 0.9 %shard_map.77 = f32[5,16,128]{2,1,0:T(8,128)} custom-call(f32[5,16,128]{2,1,0:T(8,128)S(1)} %get-tuple-element.23.cons, f32[16,128]{1,0:T(8,128)S(1)} %get-tuple-element.24.jac, f32[9,16,128]{2,1,0:T(8,128)S(1)} %get-tuple-element.25.met, s32[32,128]{1,0:T(8,128)S(1)} %get-tuple-element.26.x_index, s32[32,128]{1,0:T(8,128)S(1)} %get-tuple-element.29.z_index, ...), custom_call_target="tpu_custom_call" | custom-call | flops 1000000 | bytes 200000 | tf_op jit(solution)/shard_map/pallas_call | solution.py:613
Async XLA Ops:
  1.2 6.7 %collective-permute-start = (f32[96,128]{1,0:T(8,128)S(1)}, f32[96,128]{1,0:T(8,128)S(1)}, u32[]{:S(2)}, u32[]{:S(2)}) collective-permute-start(f32[96,128]{1,0:T(8,128)S(1)} %get-tuple-element.32), channel_id=1, source_target_pairs={{0,1},{1,2},{2,3},{3,4},{4,5},{5,6},{6,7},{7,0},{8,9},{9,10},{10,1... | collective-permute-start | bytes 147464 | tf_op jit(solution)/shard_map/ppermute | solution.py:626
  3.4 4.6 %collective-permute-start.1 = (f32[96,128]{1,0:T(8,128)S(1)}, f32[96,128]{1,0:T(8,128)S(1)}, u32[]{:S(2)}, u32[]{:S(2)}) collective-permute-start(f32[96,128]{1,0:T(8,128)S(1)} %get-tuple-element.33), channel_id=1, source_target_pairs={{1,0},{2,1},{3,2},{4,3},{5,4},{6,5},{7,6},{0,7},{9,8},{10,9},{11,1... | collective-permute-start | bytes 147464 | tf_op jit(solution)/shard_map/ppermute | solution.py:627
  8.3 3.0 %collective-permute-start.2 = (f32[88,128]{1,0:T(8,128)S(1)}, f32[88,128]{1,0:T(8,128)S(1)}, u32[]{:S(2)}, u32[]{:S(2)}) collective-permute-start(f32[88,128]{1,0:T(8,128)S(1)} %get-tuple-element.39), channel_id=1, source_target_pairs={{0,8},{8,0},{16,24},{24,16},{1,9},{9,1},{17,25},{25,17},{2,10},{10... | collective-permute-start | bytes 135176 | tf_op jit(solution)/shard_map/ppermute | solution.py:639
  9.8 3.5 %collective-permute-start.3 = (f32[88,128]{1,0:T(8,128)S(1)}, f32[88,128]{1,0:T(8,128)S(1)}, u32[]{:S(2)}, u32[]{:S(2)}) collective-permute-start(f32[88,128]{1,0:T(8,128)S(1)} %get-tuple-element.40), channel_id=1, source_target_pairs={{8,16},{16,8},{24,0},{0,24},{9,17},{17,9},{25,1},{1,25},{10,18},{1... | collective-permute-start | bytes 135176 | tf_op jit(solution)/shard_map/ppermute | solution.py:638

commit v2 on v1

v2 whole, which is shorter than its diff:
```python
import math

import jax
import jax.numpy as jnp
import numpy as np
from jax import lax
from jax.experimental import pallas as pl
from jax.experimental.pallas import tpu as pltpu
from jax.sharding import PartitionSpec as P


gamma_gas = 1.4
visc_coef = 0.1
prandtl = 0.72
lift = 6.0
heat_coef = visc_coef * gamma_gas / ((gamma_gas - 1.0) * prandtl)
vmem_bytes = 8 << 20
whole = pl.BlockSpec(memory_space=pltpu.VMEM)


def node_table():
    points = np.array([-1.0, -math.sqrt(0.2), math.sqrt(0.2), 1.0])
    scales = np.array([np.prod([points[i] - points[k] for k in range(4) if k != i]) for i in range(4)])
    table = np.zeros((4, 4))
    for i in range(4):
        for k in range(4):
            if i != k:
                table[i, k] = scales[i] / (scales[k] * (points[i] - points[k]))
        table[i, i] = -np.sum(table[i])
    return table


def weak_table():
    table = node_table()
    table[0, 0] += lift
    table[3, 3] -= lift
    return table


def rows_of(lanes):
    return lax.broadcasted_iota(jnp.int32, (8, lanes), 0)


def lanes_of(lanes):
    return lax.broadcasted_iota(jnp.int32, (8, lanes), 1)


def pick4(index, values):
    out = jnp.full(index.shape, values[3], jnp.float32)
    for k in (2, 1, 0):
        out = jnp.where(index == k, jnp.float32(values[k]), out)
    return out


def shift_weights(index, table):
    weights = {}
    for shift in range(-3, 4):
        weights[shift] = pick4(index, [table[j, j - shift] if 0 <= j - shift < 4 else 0.0 for j in range(4)])
    return weights


class Frame:
    def __init__(self, lanes):
        self.lanes = lanes
        row = rows_of(lanes)
        lane = lanes_of(lanes)
        self.row, self.lane = row, lane
        self.low_half = row < 4
        self.point_row = row % 4
        self.point_lane = lane % 4

    def deriv_weights(self):
        table = weak_table()
        self.weights_z = shift_weights(self.point_row, table)
        self.weights_y = shift_weights(self.point_lane, table)
        pair = lambda top, bottom: jnp.where(self.low_half, jnp.float32(top), jnp.float32(bottom))
        self.weights_x = [
            [
                pair(table[2 * t, 2 * s], table[2 * t + 1, 2 * s + 1]),
                pair(table[2 * t, 2 * s + 1], table[2 * t + 1, 2 * s]),
            ]
            for t in range(2)
            for s in range(2)
        ]

    def swap(self, tile):
        return pltpu.roll(tile, 4, 0)

    def deriv_x(self, pair):
        a, b = pair
        a2, b2 = self.swap(a), self.swap(b)
        w = self.weights_x
        return [
            w[2 * t][0] * a + w[2 * t][1] * a2 + w[2 * t + 1][0] * b + w[2 * t + 1][1] * b2
            for t in range(2)
        ]

    def deriv_rows(self, tile):
        out = self.weights_z[0] * tile
        for shift in (-3, -2, -1, 1, 2, 3):
            out = out + self.weights_z[shift] * pltpu.roll(tile, shift % 8, 0)
        return out

    def lane_matrix(self):
        shape = (self.lanes, self.lanes)
        to = lax.broadcasted_iota(jnp.int32, shape, 1)
        gap = to - lax.broadcasted_iota(jnp.int32, shape, 0)
        full = jnp.zeros(shape, jnp.float32)
        for shift in range(-3, 4):
            full = jnp.where(gap == shift, jnp.broadcast_to(self.weights_y[shift][0:1], shape), full)
        high = full.astype(jnp.bfloat16)
        low = (full - high.astype(jnp.float32)).astype(jnp.bfloat16)
        top = jnp.concatenate([high, low], 1)
        bottom = jnp.concatenate([high, jnp.zeros(shape, jnp.bfloat16)], 1)
        return jnp.concatenate([top, bottom], 0)

    def deriv_lanes_all(self, tiles, matrix):
        values = jnp.concatenate(tiles, 0)
        high = values.astype(jnp.bfloat16)
        low = (values - high.astype(jnp.float32)).astype(jnp.bfloat16)
        wide = jnp.dot(
            jnp.concatenate([high, low], 1), matrix, preferred_element_type=jnp.float32
        )
        out = wide[:, : self.lanes] + wide[:, self.lanes :]
        return [out[8 * i : 8 * i + 8] for i in range(len(tiles))]

    def deriv_lanes(self, tile):
        out = self.weights_y[0] * tile
        for shift in (-3, -2, -1, 1, 2, 3):
            out = out + self.weights_y[shift] * pltpu.roll(tile, shift % self.lanes, 1)
        return out

    def face_x(self, pair):
        return jnp.where(self.low_half, pair[0], pair[1])

    def face_z(self, pair, swapped=False):
        side = jnp.where(self.low_half, 3, 0) if swapped else jnp.where(self.low_half, 0, 3)
        index = side + 4 * (self.point_row % 2)
        return jnp.where(self.point_row < 2, sub_gather(pair[0], index), sub_gather(pair[1], index))

    def spread_z(self, face):
        upper = jnp.where(self.point_row == 3, 4, 0)
        inner = jnp.where(self.low_half, 0, 1)
        return [sub_gather(face, upper + inner + 2 * t) for t in range(2)]

    def sides(self, low, up):
        return jnp.where(self.low_half, jnp.float32(low), jnp.float32(up))

    def sign_lanes(self):
        return jnp.where(
            self.point_lane == 3, jnp.float32(lift), jnp.where(self.point_lane == 0, jnp.float32(-lift), 0.0)
        )

    def sign_rows(self):
        return jnp.where(
            self.point_row == 3, jnp.float32(lift), jnp.where(self.point_row == 0, jnp.float32(-lift), 0.0)
        )


def sub_gather(tile, index):
    return jnp.take_along_axis(tile, index, axis=0)


def lane_gather(tile, index):
    return jnp.take_along_axis(tile, index, axis=1)


def primitive(state):
    inverse = 1.0 / state[0]
    velocity = [state[1 + j] * inverse for j in range(3)]
    kinetic = state[1] * velocity[0] + state[2] * velocity[1] + state[3] * velocity[2]
    pressure = (gamma_gas - 1.0) * (state[4] - 0.5 * kinetic)
    return velocity, pressure, pressure * inverse


def combos(values, rows):
    w0, w1, w2, w3 = values
    m0, m1, m2 = rows
    return [
        w0 * m0,
        w1 * m1,
        w2 * m2,
        w0 * m1 + w1 * m0,
        w0 * m2 + w2 * m0,
        w1 * m2 + w2 * m1,
        w3 * m0,
        w3 * m1,
        w3 * m2,
    ]


def plain_flux(state, velocity, pressure, normal):
    speed = velocity[0] * normal[0] + velocity[1] * normal[1] + velocity[2] * normal[2]
    out = [state[0] * speed]
    for j in range(3):
        out.append(state[1 + j] * speed + pressure * normal[j])
    out.append((state[4] + pressure) * speed)
    return out, speed


def drag_flux(velocity, slopes, normal):
    m0, m1, m2 = normal
    spread = (visc_coef * 2.0 / 3.0) * (slopes[0] + slopes[1] + slopes[2])
    t00, t11, t22 = [2.0 * visc_coef * slopes[d] - spread for d in range(3)]
    t01, t02, t12 = [visc_coef * slopes[3 + d] for d in range(3)]
    stress = [
        t00 * m0 + t01 * m1 + t02 * m2,
        t01 * m0 + t11 * m1 + t12 * m2,
        t02 * m0 + t12 * m1 + t22 * m2,
    ]
    heat = heat_coef * (slopes[6] * m0 + slopes[7] * m1 + slopes[8] * m2)
    work = velocity[0] * stress[0] + velocity[1] * stress[1] + velocity[2] * stress[2]
    return stress + [work + heat], heat


def wave(speed, theta, normal_size):
    return jnp.abs(speed) + jnp.sqrt(gamma_gas * theta) * normal_size


def size_of(normal):
    return jnp.sqrt(normal[0] * normal[0] + normal[1] * normal[1] + normal[2] * normal[2])


def paired(frame, swapped_a, b):
    low = jnp.where(frame.low_half, b, swapped_a)
    up = jnp.where(frame.low_half, swapped_a, b)
    return low, up


def pack(frame, fields, low_ref, up_ref):
    fields = list(fields)
    if len(fields) % 2:
        fields.append(fields[-1])
    for g in range(len(fields) // 2):
        low, up = paired(frame, fields[2 * g], fields[2 * g + 1])
        low_ref[8 * g : 8 * g + 8, :] = low
        up_ref[8 * g : 8 * g + 8, :] = up


def unpack(frame, left_ref, right_ref, count):
    fields = []
    for g in range((count + 1) // 2):
        left = left_ref[8 * g : 8 * g + 8, :]
        right = right_ref[8 * g : 8 * g + 8, :]
        fields.append(jnp.where(frame.low_half, left, right))
        fields.append(jnp.where(frame.low_half, right, left))
    return fields[:count]


def first_of_pair(frame):
    return jnp.full((8, frame.lanes), lax.axis_index("gx") % 2) == 0


def pack_pairs(frame, fields, near_ref, far_ref):
    lower = first_of_pair(frame)
    fields = fields + [fields[-1]] * (len(fields) % 2)
    for g in range(len(fields) // 2):
        low, up = paired(frame, fields[2 * g], fields[2 * g + 1])
        near_ref[8 * g : 8 * g + 8, :] = jnp.where(lower, up, low)
        far_ref[8 * g : 8 * g + 8, :] = jnp.where(lower, low, up)


def unpack_pairs(frame, near_ref, far_ref, count):
    straight = first_of_pair(frame) == frame.low_half
    fields = []
    for g in range((count + 1) // 2):
        near = near_ref[8 * g : 8 * g + 8, :]
        far = far_ref[8 * g : 8 * g + 8, :]
        fields.append(jnp.where(straight, far, near))
        fields.append(jnp.where(straight, near, far))
    return fields[:count]


def spread_flags(frame, flags):
    count = flags.shape[-1]
    hit = lax.broadcasted_iota(jnp.int32, (count, frame.lanes), 0) == (
        lax.broadcasted_iota(jnp.int32, (count, frame.lanes), 1) // 4
    )
    wide = jnp.dot(
        flags.astype(jnp.float32), hit.astype(jnp.float32), preferred_element_type=jnp.float32
    )
    wide = (wide + 0.5).astype(jnp.int32)
    shape = (8, frame.lanes)
    return jnp.where(
        frame.low_half, jnp.broadcast_to(wide[0:1], shape), jnp.broadcast_to(wide[1:2], shape)
    )


def turn_indices(frame, code, forward_low):
    swap = (code & 4) != 0
    first = (code & 1) * 3
    second = ((code >> 1) & 1) * 3
    forward = frame.low_half if forward_low else jnp.logical_not(frame.low_half)
    flip_a = jnp.where(forward, second, first)
    flip_b = jnp.where(forward, first, second)
    row4, lane4 = frame.point_row, frame.point_lane
    lane_base = frame.lane - lane4
    row_base = frame.row - row4
    step1 = lane_base + jnp.where(swap, (lane4 - row4) & 3, lane4)
    step2 = row_base + jnp.where(swap, (lane4 - (row4 ^ flip_b)) & 3, row4 ^ first)
    step3 = lane_base + jnp.where(swap, ((lane4 ^ flip_a) + (row4 ^ flip_b)) & 3, lane4 ^ second)
    return step1, step2, step3


def turn(tile, indices):
    return lane_gather(sub_gather(lane_gather(tile, indices[0]), indices[1]), indices[2])


def store_indices(frame, ref, indices, master):
    step1, step2, step3 = indices
    stack_tiles(ref, [step1, step2, step3, frame.swap(step1), step2 ^ 4, master])


def load_indices(ref):
    step1, step2, step3, swapped1, swapped2, _ = take_tiles(ref, 0, 6)
    return (step1, step2, step3), (swapped1, swapped2, step3)


def turn_all(fields, both, first=0):
    return [turn(p, both[(first + i) % 2]) for i, p in enumerate(fields)]


def straight(frame, fields):
    return [frame.swap(p) if i % 2 else p for i, p in enumerate(fields)]


def stack_tiles(ref, tiles):
    for i, tile in enumerate(tiles):
        ref[8 * i : 8 * i + 8, :] = tile


def take_tiles(ref, first, last):
    return [ref[8 * i : 8 * i + 8, :] for i in range(first, last)]


def load_pair(ref, f):
    return [ref[f, 0:8, :], ref[f, 8:16, :]]


def load_state(ref):
    pairs = [load_pair(ref, f) for f in range(5)]
    return [[pairs[f][t] for f in range(5)] for t in range(2)]


def load_rows(ref, g):
    pairs = [load_pair(ref, 3 * g + d) for d in range(3)]
    return [[pairs[d][t] for d in range(3)] for t in range(2)]


def by_field(tiles):
    return [[tiles[0][f], tiles[1][f]] for f in range(len(tiles[0]))]


def lane_partner(frame, tile, flip):
    step = jnp.where(frame.point_lane == 3, 1, -1)
    other = lane_gather(tile, jnp.clip(frame.lane + step, 0, frame.lanes - 1))
    wall = (frame.lane == 0) | (frame.lane == frame.lanes - 1)
    return jnp.where(wall, -tile if flip else tile, other)


def lane_normal(frame, rows):
    take_before = (frame.point_lane == 0) & (frame.lane != 0)
    return [jnp.where(take_before, pltpu.roll(r, 1, 1), r) for r in rows]


def first_kernel(
    cons_in, jac_in, met_in, xm_in, xf_in, zm_in, zf_in,
    cons, jac, met, zm_out, zf_out, matrix_out, x_index, grad_out, low_out, up_out,
    xm_ref, xf_ref, sems,
):
    moves = [
        (xf_in, xf_ref),
        (zf_in, zf_out),
        (xm_in, xm_ref),
        (zm_in, zm_out),
        (cons_in, cons),
        (jac_in, jac),
        (met_in.at[0:3], met.at[0:3]),
        (met_in.at[3:6], met.at[3:6]),
        (met_in.at[6:9], met.at[6:9]),
    ]
    copies = [pltpu.make_async_copy(a, b, sems.at[i]) for i, (a, b) in enumerate(moves)]
    for c in copies:
        c.start()
    frame = Frame(cons.shape[-1])
    frame.deriv_weights()
    matrix_out[...] = frame.lane_matrix()
    for c in copies[:4]:
        c.wait()
    x_turn = turn_indices(frame, spread_flags(frame, xf_ref[...]), True)
    z_turn = turn_indices(frame, spread_flags(frame, zf_out[...]), True)
    master = spread_flags(frame, xm_ref[...])
    store_indices(frame, x_index, x_turn, master)
    for c in copies[4:]:
        c.wait()
    state = load_state(cons)
    state_f = by_field(state)
    lifted = []
    for t in range(2):
        velocity, _, theta = primitive(state[t])
        lifted.append(velocity + [theta])
    inverse = [1.0 / jac[0:8, :], 1.0 / jac[8:16, :]]
    z_turned = [turn(frame.face_z(p), z_turn) for p in state_f]
    x_turned = [turn(frame.face_x(p), x_turn) for p in state_f]
    rows = [load_rows(met, g) for g in range(3)]
    cx = by_field([combos(lifted[t], rows[0][t]) for t in range(2)])
    cz = by_field([combos(lifted[t], rows[1][t]) for t in range(2)])
    cy = by_field([combos(lifted[t], rows[2][t]) for t in range(2)])
    sign = frame.sign_lanes()
    lane_part = []
    for t in range(2):
        other = [lane_partner(frame, lifted[t][k], k < 3) for k in range(4)]
        mean = [0.5 * (lifted[t][k] + other[k]) for k in range(4)]
        lane_part.append(combos(mean, lane_normal(frame, rows[2][t])))
    grad = []
    dy = frame.deriv_lanes_all([cy[f][t] for f in range(9) for t in range(2)], matrix_out[...])
    for f in range(9):
        dx = frame.deriv_x(cx[f])
        grad.append(
            [
                dx[t]
                + frame.deriv_rows(cz[f][t])
                + dy[2 * f + t]
                + sign * lane_part[t][f]
                for t in range(2)
            ]
        )
    for f in range(9):
        for t in range(2):
            grad_out[f, 8 * t : 8 * t + 8, :] = grad[f][t]

    lead = master == 1
    own_rows = [frame.face_x(p) for p in by_field(rows[0])]
    turned_rows = [turn(p, x_turn) for p in own_rows]
    velocity, _, theta = primitive(x_turned)
    line = velocity + [theta]
    outer = (frame.point_row == 0) | (frame.point_row == 3)
    right = jnp.where(frame.point_row >= 2, 4, 0)
    picks = [right + jnp.where(frame.low_half, 3, 0), right + jnp.where(frame.low_half, 0, 3)]
    merge = lambda i, a, b: jnp.where(outer, sub_gather(a, picks[i % 2]), sub_gather(b, picks[i % 2]))
    zero = jnp.zeros_like(line[0])
    edges = [merge(0, line[0], line[1]), merge(1, line[2], line[3])]
    for d in range(3):
        edges.append(
            merge(d, jnp.where(lead, turned_rows[d], zero), jnp.where(lead, own_rows[d], zero))
        )
    faces = z_turned + [turn(frame.face_z(p), z_turn) for p in by_field(rows[1])]
    faces = [frame.swap(p) if i % 2 == 0 else p for i, p in enumerate(faces)]
    faces = faces + [
        frame.face_z(p, swapped=i % 2 == 0) for i, p in enumerate([inverse] + grad)
    ]
    pack(frame, faces + edges, low_out, up_out)


def first_cover(
    cons, jac, met, zm_ref, zf_ref, x_index, grad_in, z_index, face_out, near_out, far_out
):
    frame = Frame(cons.shape[-1])
    x_turn = load_indices(x_index)[0]
    fields = [load_pair(cons, f) for f in range(5)] + [load_pair(met, d) for d in range(3)]
    fields.append([1.0 / jac[0:8, :], 1.0 / jac[8:16, :]])
    fields = [turn(frame.face_x(p), x_turn) for p in fields]
    fields = [frame.swap(p) if i % 2 == 0 else p for i, p in enumerate(fields)]
    pack_pairs(frame, fields, near_out, far_out)
    for f in range(9):
        tile = turn(frame.face_x(load_pair(grad_in, f)), x_turn)
        face_out[8 * f : 8 * f + 8, :] = frame.swap(tile) if f % 2 == 0 else tile
    z_turn = turn_indices(frame, spread_flags(frame, zf_ref[...]), False)
    store_indices(frame, z_index, z_turn, spread_flags(frame, zm_ref[...]))


def mean_of(prim1, prim2):
    return [0.5 * (a + b) for a, b in zip(prim1[0] + [prim1[2]], prim2[0] + [prim2[2]])]


def second_kernel(
    cons, met, x_index, z_index, grad_in, x_face, left, right, grad_out, part_out, near_out, far_out
):
    frame = Frame(cons.shape[-1])
    lead = z_index[40:48, :] == 1
    x_turn = load_indices(x_index)[0]
    got = unpack(frame, left, right, 23)
    other = straight(frame, got[:8])
    own = [frame.face_z(load_pair(cons, f)) for f in range(5)]
    own_rows = [frame.face_z(load_pair(met, 3 + d)) for d in range(3)]
    normal = [jnp.where(lead, own_rows[d], other[5 + d]) for d in range(3)]
    part = combos(mean_of(primitive(own), primitive(other[:5])), normal)
    stack_tiles(part_out, part)
    across = jnp.where(frame.low_half, 0, 3) + jnp.where(frame.point_row >= 2, 4, 0)
    sign = frame.sign_rows()
    fields = take_tiles(x_face, 0, 9)
    for f in range(9):
        tile = turn(sign * sub_gather(part[f], across), x_turn)
        fields[f] = fields[f] + (frame.swap(tile) if f % 2 == 0 else tile)
    odd = frame.point_row % 2
    high = jnp.where(frame.point_row >= 2, 4, 0)

    def passed(low):
        return high + jnp.where(low, odd, 3 - odd), high + jnp.where(low, 0, 3)

    pair_a, outer_a = passed(jnp.logical_not(frame.low_half))
    pair_b, outer_b = passed(frame.low_half)
    fields.append(sub_gather(got[18], pair_b))
    fields.append(sub_gather(got[19], pair_a ^ 4))
    fields.append(
        jnp.where(odd == 0, sub_gather(got[20], outer_b), sub_gather(got[21], outer_b ^ 4))
    )
    fields.append(sub_gather(got[22], outer_a))
    pack_pairs(frame, fields, near_out, far_out)
    for f in range(9):
        spread = frame.spread_z(part[f])
        for t in range(2):
            grad_out[f, 8 * t : 8 * t + 8, :] = (
                grad_in[f, 8 * t : 8 * t + 8, :] + sign * spread[t]
            )


def plain_face(own, own_prim, other, other_prim, normal, side_sign):
    size = size_of(normal)
    flux1, speed1 = plain_flux(own, own_prim[0], own_prim[1], normal)
    flux2, speed2 = plain_flux(other, other_prim[0], other_prim[1], normal)
    fastest = jnp.maximum(wave(speed1, own_prim[2], size), wave(speed2, other_prim[2], size))
    half = 0.5 * side_sign * fastest
    return [0.5 * (flux1[c] + flux2[c]) - half * (other[c] - own[c]) for c in range(5)]


def second_cover(cons, met, z_index, lift_in, left, right, part_out, face_out, normal_out):
    frame = Frame(cons.shape[-1])
    lead = z_index[40:48, :] == 1
    both = load_indices(z_index)
    got = unpack(frame, left, right, 23)
    turned = straight(frame, got[:8]) + turn_all(got[8:18], both)
    other = turned[:5]
    other_prim = primitive(other)
    own = [frame.face_z(load_pair(cons, f)) for f in range(5)]
    own_rows = [frame.face_z(load_pair(met, 3 + d)) for d in range(3)]
    own_prim = primitive(own)
    normal = [jnp.where(lead, own_rows[d], turned[5 + d]) for d in range(3)]
    flux = plain_face(own, own_prim, other, other_prim, normal, frame.sides(-1.0, 1.0))
    sign = frame.sign_rows()
    plain_z = [frame.spread_z(flux[c]) for c in range(5)]
    face_sign = frame.sides(-lift, lift)
    slopes = [(turned[9 + f] - face_sign * lift_in[8 * f : 8 * f + 8, :]) * turned[8] for f in range(9)]
    edge_scale = turn(sign, both[0]) * turned[8]
    own_edge = jnp.where(frame.low_half, 0, 4) + jnp.where(frame.point_row >= 2, 2, 1)
    own_lines = [sub_gather(got[20 + d], own_edge ^ 4 if d == 1 else own_edge) for d in range(3)]
    stack_tiles(
        face_out,
        own_prim[0]
        + other_prim[0]
        + [other_prim[2]]
        + normal
        + drag_flux(other_prim[0], slopes, normal)[0]
        + own_lines
        + [edge_scale],
    )

    frame.deriv_weights()
    state = load_state(cons)
    rows = [load_rows(met, g) for g in range(3)]
    sign_y = frame.sign_lanes()
    up_lane = frame.point_lane == 3
    wall = (frame.lane == 0) | (frame.lane == frame.lanes - 1)
    volume = []
    lane_flux = []
    for t in range(2):
        velocity, pressure, theta = primitive(state[t])
        volume.append([plain_flux(state[t], velocity, pressure, rows[g][t])[0] for g in range(3)])
        normal = lane_normal(frame, rows[2][t])
        for d in range(3):
            normal_out[d, 8 * t : 8 * t + 8, :] = normal[d]
        half, speed = plain_flux(state[t], velocity, pressure, normal)
        own_wave = wave(speed, theta, size_of(normal))
        fastest = jnp.maximum(own_wave, lane_partner(frame, own_wave, False))
        mirrored = [-half[0], half[1], half[2], half[3], -half[4]]
        direction = jnp.where(up_lane, jnp.float32(0.5), jnp.float32(-0.5)) * fastest
        result = []
        for c in range(5):
            other_half = jnp.where(wall, mirrored[c], lane_partner(frame, half[c], False))
            other_state = lane_partner(frame, state[t][c], 1 <= c <= 3)
            result.append(0.5 * (half[c] + other_half) - direction * (other_state - state[t][c]))
        lane_flux.append(result)
    for c in range(5):
        dx = frame.deriv_x([volume[t][0][c] for t in range(2)])
        for t in range(2):
            part_out[c, 8 * t : 8 * t + 8, :] = (
                sign * plain_z[c][t]
                + dx[t]
                + frame.deriv_rows(volume[t][1][c])
                + frame.deriv_lanes(volume[t][2][c])
                + sign_y * lane_flux[t][c]
            )


def third_kernel(
    cons, jac, met, x_index, z_index, grad_in, part_in, z_face, y_normal, matrix,
    near_one, far_one, near_two, far_two, out
):
    frame = Frame(cons.shape[-1])
    frame.deriv_weights()
    state = load_state(cons)
    state_f = by_field(state)
    rows = [load_rows(met, g) for g in range(3)]
    inverse = [1.0 / jac[0:8, :], 1.0 / jac[8:16, :]]
    got = unpack_pairs(frame, near_two, far_two, 13)
    x_lead = x_index[40:48, :] == 1
    turned = straight(frame, unpack_pairs(frame, near_one, far_one, 9)) + straight(frame, got[:9])
    face_sign = frame.sides(-lift, lift)

    own = [frame.face_x(p) for p in state_f]
    own_rows = [frame.face_x(p) for p in by_field(rows[0])]
    own_prim = primitive(own)
    other = turned[:5]
    other_prim = primitive(other)
    normal_x = [jnp.where(x_lead, own_rows[d], turned[5 + d]) for d in range(3)]
    part = combos(mean_of(own_prim, other_prim), normal_x)
    slopes = []
    for f in range(9):
        lifted_part = face_sign * part[f]
        zero = jnp.zeros_like(lifted_part)
        tiles = [
            grad_in[f, 0:8, :] + jnp.where(frame.low_half, lifted_part, zero),
            grad_in[f, 8:16, :] + jnp.where(frame.low_half, zero, lifted_part),
        ]
        slopes.append([tiles[t] * inverse[t] for t in range(2)])
    own_slopes = [frame.face_x(p) for p in slopes]
    other_slopes = [(turned[9 + f] - face_sign * part[f]) * turned[8] for f in range(9)]
    flux_x = plain_face(own, own_prim, other, other_prim, normal_x, frame.sides(-1.0, 1.0))
    drag1 = drag_flux(own_prim[0], own_slopes, normal_x)[0]
    drag2 = drag_flux(other_prim[0], other_slopes, normal_x)[0]
    flux_x = [flux_x[0]] + [flux_x[1 + c] - 0.5 * (drag1[c] + drag2[c]) for c in range(4)]

    edge_a = jnp.where(frame.low_half, 0, 2) + jnp.where(frame.point_row >= 2, 4, 0)
    edge_b = edge_a + 1
    lines = [
        sub_gather(got[9], edge_a ^ 4),
        sub_gather(got[9], edge_b ^ 4),
        sub_gather(got[10], edge_a),
        sub_gather(got[10], edge_b),
        sub_gather(got[11], edge_a ^ 4),
        sub_gather(got[11], edge_b ^ 4),
        sub_gather(got[12], edge_a),
    ]
    face = take_tiles(z_face, 0, 18)
    lines[4:] = [lines[4 + d] + face[14 + d] for d in range(3)]
    z_indices = load_indices(z_index)[0]
    lines = [turn(p, z_indices) for p in lines]
    mean = [0.5 * (a + b) for a, b in zip(face[3:7], lines[:4])]
    edge_slopes = [face[17] * p for p in combos(mean, lines[4:])]
    normal_z = face[7:10]
    own_slopes = [frame.face_z(p) for p in slopes]
    drag1 = drag_flux(face[0:3], own_slopes, normal_z)[0]
    drag2 = drag_flux(face[3:6], edge_slopes, normal_z)[0]
    drag_z = [0.5 * (drag1[c] + face[10 + c] + drag2[c]) for c in range(4)]

    slopes_t = [[slopes[f][t] for f in range(9)] for t in range(2)]
    sign_y = frame.sign_lanes()
    wall = (frame.lane == 0) | (frame.lane == frame.lanes - 1)
    volume = []
    lane_flux = []
    for t in range(2):
        velocity = primitive(state[t])[0]
        volume.append([drag_flux(velocity, slopes_t[t], rows[g][t])[0] for g in range(3)])
        normal = [y_normal[d, 8 * t : 8 * t + 8, :] for d in range(3)]
        half, heat = drag_flux(velocity, slopes_t[t], normal)
        mirrored = [half[0], half[1], half[2], 2.0 * heat - half[3]]
        result = []
        for c in range(4):
            other_half = jnp.where(wall, mirrored[c], lane_partner(frame, half[c], False))
            result.append(0.5 * (half[c] + other_half))
        lane_flux.append(result)
    row_sign = frame.sign_rows()
    dy = frame.deriv_lanes_all(
        [volume[t][2][k] for k in range(4) for t in range(2)], matrix[...]
    )
    for c in range(5):
        side = face_sign * flux_x[c]
        zero = jnp.zeros_like(side)
        sides = [jnp.where(frame.low_half, side, zero), jnp.where(frame.low_half, zero, side)]
        totals = [part_in[c, 8 * t : 8 * t + 8, :] + sides[t] for t in range(2)]
        if c > 0:
            k = c - 1
            dx = frame.deriv_x([volume[t][0][k] for t in range(2)])
            spread = frame.spread_z(drag_z[k])
            for t in range(2):
                totals[t] = totals[t] - (
                    dx[t]
                    + frame.deriv_rows(volume[t][1][k])
                    + dy[2 * k + t]
                    + sign_y * lane_flux[t][k]
                    + row_sign * spread[t]
                )
        for t in range(2):
            out[c, 8 * t : 8 * t + 8, :] = -totals[t] * inverse[t]


def shaped(*shape, dtype=jnp.float32):
    return jax.ShapeDtypeStruct(shape, dtype)


def call(kernel, outs, *args, in_specs=None, scratch=()):
    return pl.pallas_call(
        kernel,
        out_shape=outs,
        in_specs=in_specs or [whole] * len(args),
        out_specs=[whole] * len(outs),
        scratch_shapes=scratch,
        compiler_params=pltpu.CompilerParams(vmem_limit_bytes=vmem_bytes),
        cost_estimate=pl.CostEstimate(flops=1_000_000, bytes_accessed=200_000, transcendentals=0),
    )(*args)


def exchange(low, up, axis):
    count = lax.axis_size(axis)
    from_left = lax.ppermute(up, axis, [(i, (i + 1) % count) for i in range(count)])
    from_right = lax.ppermute(low, axis, [((i + 1) % count, i) for i in range(count)])
    return from_left, from_right


def exchange_pairs(near, far, axis):
    count = lax.axis_size(axis)
    assert count % 2 == 0
    swaps = [[], []]
    for k in range(count):
        a, b = k, (k + 1) % count
        swaps[k % 2] += [(a, b), (b, a)]
    got_far = lax.ppermute(far, axis, swaps[1])
    got_near = lax.ppermute(near, axis, swaps[0])
    return got_near, got_far


def local(conserved, jacobian, metric, x_master, x_flip, z_master, z_flip):
    lanes = conserved.shape[-1]
    nodes = conserved.shape[1] * conserved.shape[2]
    assert conserved.shape[1:3] == (4, 4)
    cons = conserved.reshape(5, nodes, lanes)
    jac = jacobian.reshape(nodes, lanes)
    met = metric.reshape(9, nodes, lanes)
    xm, xf, zm, zf = [a.reshape(2, a.shape[-1]) for a in (x_master, x_flip, z_master, z_flip)]
    flag = (2, xm.shape[-1])
    nodal9, nodal5 = shaped(9, nodes, lanes), shaped(5, nodes, lanes)
    flags = shaped(*flag, dtype=jnp.int32)
    index = shaped(48, lanes, dtype=jnp.int32)
    matrix_shape = shaped(2 * lanes, 2 * lanes, dtype=jnp.bfloat16)
    cons, jac, met, zm, zf, matrix, x_index, grad, low_z, up_z = call(
        first_kernel,
        [nodal5, shaped(nodes, lanes), nodal9]
        + [flags] * 2
        + [matrix_shape, index, nodal9]
        + [shaped(96, lanes)] * 2,
        *[pltpu.with_memory_space_constraint(a, pltpu.HBM) for a in (cons, jac, met, xm, xf, zm, zf)],
        in_specs=[pl.BlockSpec(memory_space=pltpu.HBM)] * 7,
        scratch=[
            pltpu.VMEM(flag, jnp.int32),
            pltpu.VMEM(flag, jnp.int32),
            pltpu.SemaphoreType.DMA((9,)),
        ],
    )
    left_z, right_z = exchange(low_z, up_z, "gz")
    z_index, x_face, near_one, far_one = call(
        first_cover,
        [index, shaped(72, lanes)] + [shaped(40, lanes)] * 2,
        cons, jac, met, zm, zf, x_index, grad,
    )
    near_one, far_one = exchange_pairs(near_one, far_one, "gx")
    grad, lift_z, near_two, far_two = call(
        second_kernel,
        [nodal9, shaped(72, lanes), shaped(56, lanes), shaped(56, lanes)],
        cons, met, x_index, z_index, grad, x_face, left_z, right_z,
    )
    near_two, far_two = exchange_pairs(near_two, far_two, "gx")
    part, z_face, y_normal = call(
        second_cover,
        [nodal5, shaped(144, lanes), shaped(3, nodes, lanes)],
        cons, met, z_index, lift_z, left_z, right_z,
    )
    (rhs,) = call(
        third_kernel,
        [nodal5],
        cons, jac, met, x_index, z_index, grad, part, z_face, y_normal, matrix,
        near_one, far_one, near_two, far_two,
    )
    return rhs.reshape(conserved.shape)


def solution(mesh):
    in_specs = (
        P(None, "gx", "gz", None),
        P("gx", "gz", None),
        P(None, None, "gx", "gz", None),
        P("gx", "gz", None),
        P("gx", "gz", None),
        P("gx", "gz", None),
        P("gx", "gz", None),
    )
    out_specs = P(None, "gx", "gz", None)
    return jax.shard_map(local, mesh=mesh, in_specs=in_specs, out_specs=out_specs, check_vma=False)
```

time: 14.4 us -> 15.6 us (1.083)
  waiting for transfers between devices: 3.28 us -> 4.2 us
  starting transfers between devices: 8.06 us -> 8.58 us
  Pallas kernels: 2.81 us -> 2.6 us
    ppermute x1 -> x2, waiting for transfers between devices: 0.01 us -> 0.48 us  [exchange_pairs(): got_near = lax.ppermute(near, axis, swaps[0])]
    ppermute x1 -> x2, starting transfers between devices: 1.54 us -> 1.97 us  [exchange_pairs(): got_near = lax.ppermute(near, axis, swaps[0])]
    ppermute x1 -> x2, waiting for transfers between devices: 1.98 us -> 2.37 us  [exchange_pairs(): got_far = lax.ppermute(far, axis, swaps[1])]
    pallas_call x5, Pallas kernels: 2.81 us -> 2.6 us  [call(): pl.pallas_call(kernel, out_shape=outs, in_specs=in_specs or [whole] * len...]
    ppermute x1 -> x2, starting transfers between devices: 1.3 us -> 1.39 us  [exchange_pairs(): got_far = lax.ppermute(far, axis, swaps[1])]
  transfers between devices with their start and end apart: 4 -> 6, of which waited for: 2 -> 3; matrix products, arithmetic and copies ran while one was open for 0% -> 0% of each run, Pallas kernels for 3% -> 3%
where the time goes in v2:
time: 15.6 us; the launch traced here: 15.4 us
  starting transfers between devices  8.58 us (55%)
  waiting for transfers between devices  4.2 us (27%)
  Pallas kernels  2.6 us (17%)
    ppermute x1, starting transfers between devices, exchange(): lax.ppermute(low, axis, [((i + 1) % count, i) for i in range(count)])  3.1 us
    pallas_call x5, Pallas kernels, call(): pl.pallas_call(kernel, out_shape=outs, in_specs=in_specs or [whole] * len...  2.6 us
    ppermute x2, waiting for transfers between devices, exchange_pairs(): got_far = lax.ppermute(far, axis, swaps[1])  2.37 us
    ppermute x1, starting transfers between devices, exchange(): lax.ppermute(up, axis, [(i, (i + 1) % count) for i in range(count)])  2.11 us
    ppermute x2, starting transfers between devices, exchange_pairs(): got_near = lax.ppermute(near, axis, swaps[0])  1.97 us
    ppermute x2, starting transfers between devices, exchange_pairs(): got_far = lax.ppermute(far, axis, swaps[1])  1.39 us
    ppermute x1, waiting for transfers between devices, exchange(): lax.ppermute(up, axis, [(i, (i + 1) % count) for i in range(count)])  1.35 us
    ppermute x2, waiting for transfers between devices, exchange_pairs(): got_near = lax.ppermute(near, axis, swaps[0])  0.48 us
  transfers between devices with their start and end apart: 6, of which 3 were waited for; matrix products, arithmetic and copies ran while one was open for 0% of the time, Pallas kernels for 3%

profile of v2, /device:TPU:1, one launch (start us, length us, event | category | flops | bytes accessed | tf_op | source)
XLA Modules:
  0.0 15.4 jit_solution(2599023359149848691)
XLA Ops:
  0.0 1.2 %shard_map.73 = (f32[5,16,128]{2,1,0:T(8,128)S(1)}, f32[16,128]{1,0:T(8,128)S(1)}, f32[9,16,128]{2,1,0:T(8,128)S(1)}, s32[2,32]{1,0:T(2,128)S(1)}, s32[2,32]{1,0...) custom-call(f32[5,16,128]{2,1,0:T(8,128)} %bitcast.9, ...), custom_call_target="tpu_custom_call" | custom-call | flops 1000000 | bytes 200000 | tf_op jit(solution)/shard_map/pallas_call | solution.py:702
  1.2 2.1 %collective-permute-start = (f32[96,128]{1,0:T(8,128)S(1)}, f32[96,128]{1,0:T(8,128)S(1)}, u32[]{:S(2)}, u32[]{:S(2)}) collective-permute-start(f32[96,128]{1,0:T(8,128)S(1)} %get-tuple-element.35), channel_id=1, source_target_pairs={{0,1},{1,2},{2,3},{3,4},{4,5},{5,6},{6,7},{7,0},{8,9},{9,10},{10,1... | collective-permute-start | bytes 147464 | tf_op jit(solution)/shard_map/ppermute | solution.py:715
  3.3 3.1 %collective-permute-start.1 = (f32[96,128]{1,0:T(8,128)S(1)}, f32[96,128]{1,0:T(8,128)S(1)}, u32[]{:S(2)}, u32[]{:S(2)}) collective-permute-start(f32[96,128]{1,0:T(8,128)S(1)} %get-tuple-element.36), channel_id=1, source_target_pairs={{1,0},{2,1},{3,2},{4,3},{5,4},{6,5},{7,6},{0,7},{9,8},{10,9},{11,1... | collective-permute-start | bytes 147464 | tf_op jit(solution)/shard_map/ppermute | solution.py:716
  6.4 0.2 %shard_map.74 = (s32[48,128]{1,0:T(8,128)S(1)}, f32[72,128]{1,0:T(8,128)S(1)}, f32[40,128]{1,0:T(8,128)S(1)}, f32[40,128]{1,0:T(8,128)S(1)}) custom-call(f32[5,16,128]{2,1,0:T(8,128)S(1)} %get-tuple-element.26.cons, f32[16,128]{1,0:T(8,128)S(1)} %get-tuple-element.27.jac, f32[9,16,128]{2,1,0:T(8,128)S(1)} %get-tuple-element.28.met, ...), custom_call_target="tpu_custom_call" | custom-call | flops 1000000 | bytes 200000 | tf_op jit(solution)/shard_map/pallas_call | solution.py:702
  6.5 1.3 %collective-permute-done.left = f32[96,128]{1,0:T(8,128)S(1)} collective-permute-done((f32[96,128]{1,0:T(8,128)S(1)}, f32[96,128]{1,0:T(8,128)S(1)}, u32[]{:S(2)}, u32[]{:S(2)}) %collective-permute-start) | collective-permute-done | bytes 49184 | tf_op jit(solution)/shard_map/ppermute | solution.py:715
  7.9 0.0 collective-permute-done.1.right
  7.9 0.2 %shard_map.75 = (f32[9,16,128]{2,1,0:T(8,128)S(1)}, f32[72,128]{1,0:T(8,128)S(1)}, f32[56,128]{1,0:T(8,128)S(1)}, f32[56,128]{1,0:T(8,128)S(1)}) custom-call(f32[5,16,128]{2,1,0:T(8,128)S(1)} %get-tuple-element.26.cons, f32[9,16,128]{2,1,0:T(8,128)S(1)} %get-tuple-element.28.met, s32[48,128]{1,0:T(8,128)S(1)} %get-tuple-element.29.x_index, ...), custom_call_target="tpu_custom_call" | custom-call | flops 1000000 | bytes 200000 | tf_op jit(solution)/shard_map/pallas_call | solution.py:702
  8.1 1.5 %collective-permute-start.4 = (f32[56,128]{1,0:T(8,128)S(1)}, f32[56,128]{1,0:T(8,128)S(1)}, u32[]{:S(2)}, u32[]{:S(2)}) collective-permute-start(f32[56,128]{1,0:T(8,128)S(1)} %get-tuple-element.45), channel_id=1, source_target_pairs={{0,8},{8,0},{16,24},{24,16},{1,9},{9,1},{17,25},{25,17},{2,10},{10... | collective-permute-start | bytes 86024 | tf_op jit(solution)/shard_map/ppermute | solution.py:728
  9.6 1.3 %collective-permute-start.5 = (f32[56,128]{1,0:T(8,128)S(1)}, f32[56,128]{1,0:T(8,128)S(1)}, u32[]{:S(2)}, u32[]{:S(2)}) collective-permute-start(f32[56,128]{1,0:T(8,128)S(1)} %get-tuple-element.46), channel_id=1, source_target_pairs={{8,16},{16,8},{24,0},{0,24},{9,17},{17,9},{25,1},{1,25},{10,18},{1... | collective-permute-start | bytes 86024 | tf_op jit(solution)/shard_map/ppermute | solution.py:727
  10.9 0.4 %collective-permute-start.2 = (f32[40,128]{1,0:T(8,128)S(1)}, f32[40,128]{1,0:T(8,128)S(1)}, u32[]{:S(2)}, u32[]{:S(2)}) collective-permute-start(f32[40,128]{1,0:T(8,128)S(1)} %get-tuple-element.43), channel_id=1, source_target_pairs={{0,8},{8,0},{16,24},{24,16},{1,9},{9,1},{17,25},{25,17},{2,10},{10... | collective-permute-start | bytes 61448 | tf_op jit(solution)/shard_map/ppermute | solution.py:728
  11.3 0.1 collective-permute-start.3
  11.4 0.3 %shard_map.76 = (f32[5,16,128]{2,1,0:T(8,128)S(1)}, f32[144,128]{1,0:T(8,128)S(1)}, f32[3,16,128]{2,1,0:T(8,128)S(1)}) custom-call(f32[5,16,128]{2,1,0:T(8,128)S(1)} %get-tuple-element.26.cons, f32[9,16,128]{2,1,0:T(8,128)S(1)} %get-tuple-element.28.met, s32[48,128]{1,0:T(8,128)S(1)} %get-tuple-element.33.z_index, f32[72,128]{1,0:T(8,128)S(1)} %get-tuple-element.38.lift_in, ...), custom_call_target="tpu_custom_call" | custom-call | flops 1000000 | bytes 200000 | tf_op jit(solution)/shard_map/pallas_call | solution.py:702
  11.7 0.5 %collective-permute-done.2.near_one = f32[40,128]{1,0:T(8,128)S(1)} collective-permute-done((f32[40,128]{1,0:T(8,128)S(1)}, f32[40,128]{1,0:T(8,128)S(1)}, u32[]{:S(2)}, u32[]{:S(2)}) %collective-permute-start.2) | collective-permute-done | bytes 20512 | tf_op jit(solution)/shard_map/ppermute | solution.py:728
  12.2 2.4 %collective-permute-done.3.far_one = f32[40,128]{1,0:T(8,128)S(1)} collective-permute-done((f32[40,128]{1,0:T(8,128)S(1)}, f32[40,128]{1,0:T(8,128)S(1)}, u32[]{:S(2)}, u32[]{:S(2)}) %collective-permute-start.3) | collective-permute-done | bytes 20512 | tf_op jit(solution)/shard_map/ppermute | solution.py:727
  14.6 0.0 collective-permute-done.4.near_two
  14.6 0.0 collective-permute-done.5.far_two
  14.6 0.8 %shard_map.77 = f32[5,16,128]{2,1,0:T(8,128)} custom-call(f32[5,16,128]{2,1,0:T(8,128)S(1)} %get-tuple-element.26.cons, f32[16,128]{1,0:T(8,128)S(1)} %get-tuple-element.27.jac, f32[9,16,128]{2,1,0:T(8,128)S(1)} %get-tuple-element.28.met, s32[48,128]{1,0:T(8,128)S(1)} %get-tuple-element.29.x_index, s32[48,128]{1,0:T(8,128)S(1)} %get-tuple-element.33.z_index, ...), custom_call_target="tpu_custom_call" | custom-call | flops 1000000 | bytes 200000 | tf_op jit(solution)/shard_map/pallas_call | solution.py:702
Async XLA Ops:
  1.2 6.7 %collective-permute-start = (f32[96,128]{1,0:T(8,128)S(1)}, f32[96,128]{1,0:T(8,128)S(1)}, u32[]{:S(2)}, u32[]{:S(2)}) collective-permute-start(f32[96,128]{1,0:T(8,128)S(1)} %get-tuple-element.35), channel_id=1, source_target_pairs={{0,1},{1,2},{2,3},{3,4},{4,5},{5,6},{6,7},{7,0},{8,9},{9,10},{10,1... | collective-permute-start | bytes 147464 | tf_op jit(solution)/shard_map/ppermute | solution.py:715
  3.3 4.6 %collective-permute-start.1 = (f32[96,128]{1,0:T(8,128)S(1)}, f32[96,128]{1,0:T(8,128)S(1)}, u32[]{:S(2)}, u32[]{:S(2)}) collective-permute-start(f32[96,128]{1,0:T(8,128)S(1)} %get-tuple-element.36), channel_id=1, source_target_pairs={{1,0},{2,1},{3,2},{4,3},{5,4},{6,5},{7,6},{0,7},{9,8},{10,9},{11,1... | collective-permute-start | bytes 147464 | tf_op jit(solution)/shard_map/ppermute | solution.py:716
  8.1 6.5 %collective-permute-start.4 = (f32[56,128]{1,0:T(8,128)S(1)}, f32[56,128]{1,0:T(8,128)S(1)}, u32[]{:S(2)}, u32[]{:S(2)}) collective-permute-start(f32[56,128]{1,0:T(8,128)S(1)} %get-tuple-element.45), channel_id=1, source_target_pairs={{0,8},{8,0},{16,24},{24,16},{1,9},{9,1},{17,25},{25,17},{2,10},{10... | collective-permute-start | bytes 86024 | tf_op jit(solution)/shard_map/ppermute | solution.py:728
  9.6 4.9 %collective-permute-start.5 = (f32[56,128]{1,0:T(8,128)S(1)}, f32[56,128]{1,0:T(8,128)S(1)}, u32[]{:S(2)}, u32[]{:S(2)}) collective-permute-start(f32[56,128]{1,0:T(8,128)S(1)} %get-tuple-element.46), channel_id=1, source_target_pairs={{8,16},{16,8},{24,0},{0,24},{9,17},{17,9},{25,1},{1,25},{10,18},{1... | collective-permute-start | bytes 86024 | tf_op jit(solution)/shard_map/ppermute | solution.py:727
  10.9 1.3 %collective-permute-start.2 = (f32[40,128]{1,0:T(8,128)S(1)}, f32[40,128]{1,0:T(8,128)S(1)}, u32[]{:S(2)}, u32[]{:S(2)}) collective-permute-start(f32[40,128]{1,0:T(8,128)S(1)} %get-tuple-element.43), channel_id=1, source_target_pairs={{0,8},{8,0},{16,24},{24,16},{1,9},{9,1},{17,25},{25,17},{2,10},{10... | collective-permute-start | bytes 61448 | tf_op jit(solution)/shard_map/ppermute | solution.py:728
  11.3 3.2 %collective-permute-start.3 = (f32[40,128]{1,0:T(8,128)S(1)}, f32[40,128]{1,0:T(8,128)S(1)}, u32[]{:S(2)}, u32[]{:S(2)}) collective-permute-start(f32[40,128]{1,0:T(8,128)S(1)} %get-tuple-element.44), channel_id=1, source_target_pairs={{8,16},{16,8},{24,0},{0,24},{9,17},{17,9},{25,1},{1,25},{10,18},{1... | collective-permute-start | bytes 61448 | tf_op jit(solution)/shard_map/ppermute | solution.py:727

commit v3 on v2

--- a/solution.py
+++ b/solution.py
@@ -57,6 +57,15 @@
     for shift in range(-3, 4):
         weights[shift] = pick4(index, [table[j, j - shift] if 0 <= j - shift < 4 else 0.0 for j in range(4)])
     return weights
+
+
+def three_parts(values):
+    parts = []
+    for _ in range(3):
+        part = values.astype(jnp.bfloat16)
+        values = values - part.astype(jnp.float32)
+        parts.append(part)
+    return parts
 
 
 class Frame:
@@ -108,20 +117,21 @@
         full = jnp.zeros(shape, jnp.float32)
         for shift in range(-3, 4):
             full = jnp.where(gap == shift, jnp.broadcast_to(self.weights_y[shift][0:1], shape), full)
-        high = full.astype(jnp.bfloat16)
-        low = (full - high.astype(jnp.float32)).astype(jnp.bfloat16)
-        top = jnp.concatenate([high, low], 1)
-        bottom = jnp.concatenate([high, jnp.zeros(shape, jnp.bfloat16)], 1)
+        high, middle, low = three_parts(full)
+        top = jnp.concatenate([high, middle, high], 1)
+        bottom = jnp.concatenate([high, middle, low], 1)
         return jnp.concatenate([top, bottom], 0)
 
     def deriv_lanes_all(self, tiles, matrix):
-        values = jnp.concatenate(tiles, 0)
-        high = values.astype(jnp.bfloat16)
-        low = (values - high.astype(jnp.float32)).astype(jnp.bfloat16)
+        high, middle, low = three_parts(jnp.concatenate(tiles, 0))
+        n = self.lanes
         wide = jnp.dot(
-            jnp.concatenate([high, low], 1), matrix, preferred_element_type=jnp.float32
+            jnp.concatenate([high, middle], 1), matrix[:, : 2 * n], preferred_element_type=jnp.float32
         )
-        out = wide[:, : self.lanes] + wide[:, self.lanes :]
+        rest = jnp.dot(
+            jnp.concatenate([low, high], 1), matrix[:, 2 * n :], preferred_element_type=jnp.float32
+        )
+        out = wide[:, :n] + (wide[:, n:] + rest)
         return [out[8 * i : 8 * i + 8] for i in range(len(tiles))]
 
     def deriv_lanes(self, tile):
@@ -198,19 +208,27 @@
     return out, speed
 
 
-def drag_flux(velocity, slopes, normal):
+def traction(slopes, normal):
     m0, m1, m2 = normal
     spread = (visc_coef * 2.0 / 3.0) * (slopes[0] + slopes[1] + slopes[2])
     t00, t11, t22 = [2.0 * visc_coef * slopes[d] - spread for d in range(3)]
     t01, t02, t12 = [visc_coef * slopes[3 + d] for d in range(3)]
-    stress = [
+    return [
         t00 * m0 + t01 * m1 + t02 * m2,
         t01 * m0 + t11 * m1 + t12 * m2,
         t02 * m0 + t12 * m1 + t22 * m2,
+        heat_coef * (slopes[6] * m0 + slopes[7] * m1 + slopes[8] * m2),
     ]
-    heat = heat_coef * (slopes[6] * m0 + slopes[7] * m1 + slopes[8] * m2)
-    work = velocity[0] * stress[0] + velocity[1] * stress[1] + velocity[2] * stress[2]
-    return stress + [work + heat], heat
+
+
+def drag_of(velocity, forces):
+    work = velocity[0] * forces[0] + velocity[1] * forces[1] + velocity[2] * forces[2]
+    return forces[:3] + [work + forces[3]]
+
+
+def drag_flux(velocity, slopes, normal):
+    forces = traction(slopes, normal)
+    return drag_of(velocity, forces), forces[3]
 
 
 def wave(speed, theta, normal_size):
@@ -363,36 +381,32 @@
     return [jnp.where(take_before, pltpu.roll(r, 1, 1), r) for r in rows]
 
 
+def split_nodal(nodal):
+    return nodal.at[0:5], nodal.at[5], nodal.at[6:15]
+
+
 def first_kernel(
     cons_in, jac_in, met_in, xm_in, xf_in, zm_in, zf_in,
-    cons, jac, met, zm_out, zf_out, matrix_out, x_index, grad_out, low_out, up_out,
-    xm_ref, xf_ref, sems,
+    nodal, flags, matrix_out, x_index, grad_out, low_out, up_out, sems,
 ):
-    moves = [
-        (xf_in, xf_ref),
-        (zf_in, zf_out),
-        (xm_in, xm_ref),
-        (zm_in, zm_out),
-        (cons_in, cons),
-        (jac_in, jac),
-        (met_in.at[0:3], met.at[0:3]),
-        (met_in.at[3:6], met.at[3:6]),
-        (met_in.at[6:9], met.at[6:9]),
-    ]
-    copies = [pltpu.make_async_copy(a, b, sems.at[i]) for i, (a, b) in enumerate(moves)]
-    for c in copies:
-        c.start()
+    cons, jac, met = split_nodal(nodal)
+    flag_moves = [(a, flags.at[i]) for i, a in enumerate((xf_in, zf_in, xm_in, zm_in))]
+    moves = [(cons_in, cons), (jac_in, jac)]
+    moves += [(met_in.at[3 * g : 3 * g + 3], met.at[3 * g : 3 * g + 3]) for g in range(3)]
+    for a, b in flag_moves:
+        pltpu.make_async_copy(a, b, sems.at[0]).start()
+    for a, b in moves:
+        pltpu.make_async_copy(a, b, sems.at[1]).start()
     frame = Frame(cons.shape[-1])
     frame.deriv_weights()
     matrix_out[...] = frame.lane_matrix()
-    for c in copies[:4]:
-        c.wait()
-    x_turn = turn_indices(frame, spread_flags(frame, xf_ref[...]), True)
-    z_turn = turn_indices(frame, spread_flags(frame, zf_out[...]), True)
-    master = spread_flags(frame, xm_ref[...])
+    pltpu.make_async_copy(flags, flags, sems.at[0]).wait()
+    x_turn = turn_indices(frame, spread_flags(frame, flags[0]), True)
+    z_turn = turn_indices(frame, spread_flags(frame, flags[1]), True)
+    master = spread_flags(frame, flags[2])
     store_indices(frame, x_index, x_turn, master)
-    for c in copies[4:]:
-        c.wait()
+    z_lead = spread_flags(frame, flags[3]) == 1
+    pltpu.make_async_copy(nodal, nodal, sems.at[1]).wait()
     state = load_state(cons)
     state_f = by_field(state)
     lifted = []
@@ -439,22 +453,24 @@
     picks = [right + jnp.where(frame.low_half, 3, 0), right + jnp.where(frame.low_half, 0, 3)]
     merge = lambda i, a, b: jnp.where(outer, sub_gather(a, picks[i % 2]), sub_gather(b, picks[i % 2]))
     zero = jnp.zeros_like(line[0])
-    edges = [merge(0, line[0], line[1]), merge(1, line[2], line[3])]
+    edges = [merge(1, line[0], line[1]), merge(0, line[2], line[3])]
     for d in range(3):
         edges.append(
-            merge(d, jnp.where(lead, turned_rows[d], zero), jnp.where(lead, own_rows[d], zero))
+            merge(d + 1, jnp.where(lead, turned_rows[d], zero), jnp.where(lead, own_rows[d], zero))
         )
-    faces = z_turned + [turn(frame.face_z(p), z_turn) for p in by_field(rows[1])]
+    z_rows = [frame.face_z(p) for p in by_field(rows[1])]
+    slots = [frame.face_z(p) for p in grad]
+    known = [turn(p, z_turn) for p in z_rows] + traction(slots, z_rows)
+    slots = [jnp.where(z_lead, a, b) for a, b in zip(known, slots)] + slots[7:]
+    faces = z_turned + [frame.face_z(inverse)] + slots
     faces = [frame.swap(p) if i % 2 == 0 else p for i, p in enumerate(faces)]
-    faces = faces + [
-        frame.face_z(p, swapped=i % 2 == 0) for i, p in enumerate([inverse] + grad)
-    ]
     pack(frame, faces + edges, low_out, up_out)
 
 
 def first_cover(
-    cons, jac, met, zm_ref, zf_ref, x_index, grad_in, z_index, face_out, near_out, far_out
+    nodal, flags, x_index, grad_in, z_index, x_back, face_out, near_out, far_out
 ):
+    cons, jac, met = split_nodal(nodal)
     frame = Frame(cons.shape[-1])
     x_turn = load_indices(x_index)[0]
     fields = [load_pair(cons, f) for f in range(5)] + [load_pair(met, d) for d in range(3)]
@@ -463,10 +479,12 @@
     fields = [frame.swap(p) if i % 2 == 0 else p for i, p in enumerate(fields)]
     pack_pairs(frame, fields, near_out, far_out)
     for f in range(9):
-        tile = turn(frame.face_x(load_pair(grad_in, f)), x_turn)
+        tile = frame.face_x(load_pair(grad_in, f))
         face_out[8 * f : 8 * f + 8, :] = frame.swap(tile) if f % 2 == 0 else tile
-    z_turn = turn_indices(frame, spread_flags(frame, zf_ref[...]), False)
-    store_indices(frame, z_index, z_turn, spread_flags(frame, zm_ref[...]))
+    z_turn = turn_indices(frame, spread_flags(frame, flags[1]), False)
+    store_indices(frame, z_index, z_turn, spread_flags(frame, flags[3]))
+    x_return = turn_indices(frame, spread_flags(frame, flags[0]), False)
+    store_indices(frame, x_back, x_return, take_tiles(x_index, 5, 6)[0])
 
 
 def mean_of(prim1, prim2):
@@ -474,24 +492,25 @@
 
 
 def second_kernel(
-    cons, met, x_index, z_index, grad_in, x_face, left, right, grad_out, part_out, near_out, far_out
+    nodal, z_index, grad_in, x_face, near_in, left, right,
+    grad_out, part_out, near_out, far_out
 ):
+    cons, _, met = split_nodal(nodal)
     frame = Frame(cons.shape[-1])
     lead = z_index[40:48, :] == 1
-    x_turn = load_indices(x_index)[0]
-    got = unpack(frame, left, right, 23)
-    other = straight(frame, got[:8])
+    got = unpack(frame, left, right, 20)
+    other = straight(frame, got[:9])
     own = [frame.face_z(load_pair(cons, f)) for f in range(5)]
     own_rows = [frame.face_z(load_pair(met, 3 + d)) for d in range(3)]
-    normal = [jnp.where(lead, own_rows[d], other[5 + d]) for d in range(3)]
+    normal = [jnp.where(lead, own_rows[d], other[6 + d]) for d in range(3)]
     part = combos(mean_of(primitive(own), primitive(other[:5])), normal)
     stack_tiles(part_out, part)
-    across = jnp.where(frame.low_half, 0, 3) + jnp.where(frame.point_row >= 2, 4, 0)
+    right = jnp.where(frame.point_row >= 2, 4, 0)
+    across = [right + jnp.where(frame.low_half, 3, 0), right + jnp.where(frame.low_half, 0, 3)]
     sign = frame.sign_rows()
     fields = take_tiles(x_face, 0, 9)
     for f in range(9):
-        tile = turn(sign * sub_gather(part[f], across), x_turn)
-        fields[f] = fields[f] + (frame.swap(tile) if f % 2 == 0 else tile)
+        fields[f] = fields[f] + sign * sub_gather(part[f], across[f % 2])
     odd = frame.point_row % 2
     high = jnp.where(frame.point_row >= 2, 4, 0)
 
@@ -500,13 +519,15 @@
 
     pair_a, outer_a = passed(jnp.logical_not(frame.low_half))
     pair_b, outer_b = passed(frame.low_half)
-    fields.append(sub_gather(got[18], pair_b))
-    fields.append(sub_gather(got[19], pair_a ^ 4))
+    fields.append(sub_gather(got[15], pair_b ^ 4))
+    fields.append(sub_gather(got[16], pair_a))
     fields.append(
-        jnp.where(odd == 0, sub_gather(got[20], outer_b), sub_gather(got[21], outer_b ^ 4))
-    )
-    fields.append(sub_gather(got[22], outer_a))
-    pack_pairs(frame, fields, near_out, far_out)
+        jnp.where(odd == 0, sub_gather(got[17], outer_b ^ 4), sub_gather(got[18], outer_b))
+    )
+    fields.append(sub_gather(got[19], outer_a ^ 4))
+    static = near_in.shape[0]
+    near_out[:static, :] = near_in[...]
+    pack_pairs(frame, fields, near_out.at[static:], far_out)
     for f in range(9):
         spread = frame.spread_z(part[f])
         for t in range(2):
@@ -524,33 +545,37 @@
     return [0.5 * (flux1[c] + flux2[c]) - half * (other[c] - own[c]) for c in range(5)]
 
 
-def second_cover(cons, met, z_index, lift_in, left, right, part_out, face_out, normal_out):
+def second_cover(nodal, z_index, lift_in, left, right, part_out, face_out, normal_out):
+    cons, _, met = split_nodal(nodal)
     frame = Frame(cons.shape[-1])
     lead = z_index[40:48, :] == 1
     both = load_indices(z_index)
-    got = unpack(frame, left, right, 23)
-    turned = straight(frame, got[:8]) + turn_all(got[8:18], both)
+    got = unpack(frame, left, right, 20)
+    turned = straight(frame, got[:9])
+    scale, *slots = turn_all(got[5:15], both, 5)
     other = turned[:5]
     other_prim = primitive(other)
     own = [frame.face_z(load_pair(cons, f)) for f in range(5)]
     own_rows = [frame.face_z(load_pair(met, 3 + d)) for d in range(3)]
     own_prim = primitive(own)
-    normal = [jnp.where(lead, own_rows[d], turned[5 + d]) for d in range(3)]
+    normal = [jnp.where(lead, own_rows[d], turned[6 + d]) for d in range(3)]
     flux = plain_face(own, own_prim, other, other_prim, normal, frame.sides(-1.0, 1.0))
     sign = frame.sign_rows()
     plain_z = [frame.spread_z(flux[c]) for c in range(5)]
     face_sign = frame.sides(-lift, lift)
-    slopes = [(turned[9 + f] - face_sign * lift_in[8 * f : 8 * f + 8, :]) * turned[8] for f in range(9)]
-    edge_scale = turn(sign, both[0]) * turned[8]
+    forces = [jnp.where(lead, a, b) for a, b in zip(traction(slots, normal), slots[3:7])]
+    lifts = traction([face_sign * p for p in take_tiles(lift_in, 0, 9)], normal)
+    forces = [scale * (a - b) for a, b in zip(forces, lifts)]
+    edge_scale = turn(sign, both[0]) * scale
     own_edge = jnp.where(frame.low_half, 0, 4) + jnp.where(frame.point_row >= 2, 2, 1)
-    own_lines = [sub_gather(got[20 + d], own_edge ^ 4 if d == 1 else own_edge) for d in range(3)]
+    own_lines = [sub_gather(got[17 + d], own_edge if d == 1 else own_edge ^ 4) for d in range(3)]
     stack_tiles(
         face_out,
         own_prim[0]
         + other_prim[0]
         + [other_prim[2]]
         + normal
-        + drag_flux(other_prim[0], slopes, normal)[0]
+        + drag_of(other_prim[0], forces)
         + own_lines
         + [edge_scale],
     )
@@ -593,18 +618,21 @@
 
 
 def third_kernel(
-    cons, jac, met, x_index, z_index, grad_in, part_in, z_face, y_normal, matrix,
-    near_one, far_one, near_two, far_two, out
+    nodal, x_index, z_index, grad_in, part_in, z_face, y_normal, matrix,
+    far_one, near_two, far_two, out
 ):
+    cons, jac, met = split_nodal(nodal)
     frame = Frame(cons.shape[-1])
     frame.deriv_weights()
     state = load_state(cons)
     state_f = by_field(state)
     rows = [load_rows(met, g) for g in range(3)]
     inverse = [1.0 / jac[0:8, :], 1.0 / jac[8:16, :]]
-    got = unpack_pairs(frame, near_two, far_two, 13)
+    static = far_one.shape[0]
+    got = unpack_pairs(frame, near_two.at[static:], far_two, 13)
     x_lead = x_index[40:48, :] == 1
-    turned = straight(frame, unpack_pairs(frame, near_one, far_one, 9)) + straight(frame, got[:9])
+    turned = straight(frame, unpack_pairs(frame, near_two.at[:static], far_one, 9))
+    turned = turned + turn_all(got[:9], load_indices(x_index))
     face_sign = frame.sides(-lift, lift)
 
     own = [frame.face_x(p) for p in state_f]
@@ -717,16 +745,14 @@
     return from_left, from_right
 
 
-def exchange_pairs(near, far, axis):
+def exchange_pairs(values, axis, far):
     count = lax.axis_size(axis)
     assert count % 2 == 0
-    swaps = [[], []]
-    for k in range(count):
+    swaps = []
+    for k in range(far, count, 2):
         a, b = k, (k + 1) % count
-        swaps[k % 2] += [(a, b), (b, a)]
-    got_far = lax.ppermute(far, axis, swaps[1])
-    got_near = lax.ppermute(near, axis, swaps[0])
-    return got_near, got_far
+        swaps += [(a, b), (b, a)]
+    return lax.ppermute(values, axis, swaps)
 
 
 def local(conserved, jacobian, metric, x_master, x_flip, z_master, z_flip):
@@ -739,46 +765,47 @@
     xm, xf, zm, zf = [a.reshape(2, a.shape[-1]) for a in (x_master, x_flip, z_master, z_flip)]
     flag = (2, xm.shape[-1])
     nodal9, nodal5 = shaped(9, nodes, lanes), shaped(5, nodes, lanes)
-    flags = shaped(*flag, dtype=jnp.int32)
     index = shaped(48, lanes, dtype=jnp.int32)
-    matrix_shape = shaped(2 * lanes, 2 * lanes, dtype=jnp.bfloat16)
-    cons, jac, met, zm, zf, matrix, x_index, grad, low_z, up_z = call(
+    matrix_shape = shaped(2 * lanes, 3 * lanes, dtype=jnp.bfloat16)
+    nodal, flags, matrix, x_index, grad, low_z, up_z = call(
         first_kernel,
-        [nodal5, shaped(nodes, lanes), nodal9]
-        + [flags] * 2
-        + [matrix_shape, index, nodal9]
-        + [shaped(96, lanes)] * 2,
+        [
+            shaped(15, nodes, lanes),
+            shaped(4, *flag, dtype=jnp.int32),
+            matrix_shape,
+            index,
+            nodal9,
+            shaped(80, lanes),
+            shaped(80, lanes),
+        ],
         *[pltpu.with_memory_space_constraint(a, pltpu.HBM) for a in (cons, jac, met, xm, xf, zm, zf)],
         in_specs=[pl.BlockSpec(memory_space=pltpu.HBM)] * 7,
-        scratch=[
-            pltpu.VMEM(flag, jnp.int32),
-            pltpu.VMEM(flag, jnp.int32),
-            pltpu.SemaphoreType.DMA((9,)),
-        ],
+        scratch=[pltpu.SemaphoreType.DMA((2,))],
     )
     left_z, right_z = exchange(low_z, up_z, "gz")
-    z_index, x_face, near_one, far_one = call(
+    z_index, x_back, x_face, near_one, far_one = call(
         first_cover,
-        [index, shaped(72, lanes)] + [shaped(40, lanes)] * 2,
-        cons, jac, met, zm, zf, x_index, grad,
-    )
-    near_one, far_one = exchange_pairs(near_one, far_one, "gx")
+        [index, index, shaped(72, lanes)] + [shaped(40, lanes)] * 2,
+        nodal, flags, x_index, grad,
+    )
+    far_one = exchange_pairs(far_one, "gx", 1)
     grad, lift_z, near_two, far_two = call(
         second_kernel,
-        [nodal9, shaped(72, lanes), shaped(56, lanes), shaped(56, lanes)],
-        cons, met, x_index, z_index, grad, x_face, left_z, right_z,
-    )
-    near_two, far_two = exchange_pairs(near_two, far_two, "gx")
+        [nodal9, shaped(72, lanes), shaped(96, lanes), shaped(56, lanes)],
+        nodal, z_index, grad, x_face, near_one, left_z, right_z,
+    )
+    far_two = exchange_pairs(far_two, "gx", 1)
+    near_two = exchange_pairs(near_two, "gx", 0)
     part, z_face, y_normal = call(
         second_cover,
         [nodal5, shaped(144, lanes), shaped(3, nodes, lanes)],
-        cons, met, z_index, lift_z, left_z, right_z,
+        nodal, z_index, lift_z, left_z, right_z,
     )
     (rhs,) = call(
         third_kernel,
         [nodal5],
-        cons, jac, met, x_index, z_index, grad, part, z_face, y_normal, matrix,
-        near_one, far_one, near_two, far_two,
+        nodal, x_back, z_index, grad, part, z_face, y_normal, matrix,
+        far_one, near_two, far_two,
     )
     return rhs.reshape(conserved.shape)
 

time: 15.6 us -> 15.3 us (0.981)
  the two profiles are of different devices: /device:TPU:1 before, /device:TPU:0 now
where the time goes in v3:
time: 15.3 us; the launch traced here: 15.1 us
  starting transfers between devices  8.03 us (52%)
  waiting for transfers between devices  4.65 us (30%)
  Pallas kernels  2.43 us (16%)
    ppermute x1, starting transfers between devices, exchange(): lax.ppermute(low, axis, [((i + 1) % count, i) for i in range(count)])  3.1 us
    ppermute x1, starting transfers between devices, exchange(): lax.ppermute(up, axis, [(i, (i + 1) % count) for i in range(count)])  3.05 us
    ppermute x3, waiting for transfers between devices, exchange_pairs(): return lax.ppermute(values, axis, swaps)  2.89 us
    pallas_call x5, Pallas kernels, call(): pl.pallas_call(kernel, out_shape=outs, in_specs=in_specs or [whole] * len...  2.43 us
    ppermute x3, starting transfers between devices, exchange_pairs(): return lax.ppermute(values, axis, swaps)  1.88 us
    ppermute x1, waiting for transfers between devices, exchange(): lax.ppermute(up, axis, [(i, (i + 1) % count) for i in range(count)])  1.76 us
  transfers between devices with their start and end apart: 5, of which 2 were waited for; matrix products, arithmetic and copies ran while one was open for 0% of the time, Pallas kernels for 3%

profile of v3, /device:TPU:0, one launch (start us, length us, event | category | flops | bytes accessed | tf_op | source)
XLA Modules:
  0.0 15.1 jit_solution(4160575696997145270)
XLA Ops:
  0.0 1.1 %shard_map.73 = (f32[15,16,128]{2,1,0:T(8,128)S(1)}, s32[4,2,32]{2,1,0:T(2,128)S(1)}, bf16[256,384]{1,0:T(8,128)(2,1)S(1)}, s32[48,128]{1,0:T(8,128)S(1)}, f32[9...) custom-call(f32[5,16,128]{2,1,0:T(8,128)} %bitcast.9, f32[16,128]{1,0:T(8,128)} %bitcast.10, ...), custom_call_target="tpu_custom_call" | custom-call | flops 1000000 | bytes 200000 | tf_op jit(solution)/shard_map/pallas_call | solution.py:730
  1.1 3.1 %collective-permute-start = (f32[80,128]{1,0:T(8,128)S(1)}, f32[80,128]{1,0:T(8,128)S(1)}, u32[]{:S(2)}, u32[]{:S(2)}) collective-permute-start(f32[80,128]{1,0:T(8,128)S(1)} %get-tuple-element.32), channel_id=1, source_target_pairs={{0,1},{1,2},{2,3},{3,4},{4,5},{5,6},{6,7},{7,0},{8,9},{9,10},{10,1... | collective-permute-start | bytes 122888 | tf_op jit(solution)/shard_map/ppermute | solution.py:743
  4.2 3.1 %collective-permute-start.1 = (f32[80,128]{1,0:T(8,128)S(1)}, f32[80,128]{1,0:T(8,128)S(1)}, u32[]{:S(2)}, u32[]{:S(2)}) collective-permute-start(f32[80,128]{1,0:T(8,128)S(1)} %get-tuple-element.33), channel_id=1, source_target_pairs={{1,0},{2,1},{3,2},{4,3},{5,4},{6,5},{7,6},{0,7},{9,8},{10,9},{11,1... | collective-permute-start | bytes 122888 | tf_op jit(solution)/shard_map/ppermute | solution.py:744
  7.3 0.2 %shard_map.74 = (s32[48,128]{1,0:T(8,128)S(1)}, s32[48,128]{1,0:T(8,128)S(1)}, f32[72,128]{1,0:T(8,128)S(1)}, f32[40,128]{1,0:T(8,128)S(1)}, f32[40,128]{1,0:T(8,128)S(1)}) custom-call(f32[15,16,128]{2,1,0:T(8,128)S(1)} %get-tuple-element.24.nodal, s32[4,2,32]{2,1,0:T(2,128)S(1)} %get-tuple-element.25.flags, s32[48,128]{1,0:T(8,128)S(1)} %get-tuple-element.26.x_index, ...), custom_call_target="tpu_custom_call" | custom-call | flops 1000000 | bytes 200000 | tf_op jit(solution)/shard_map/pallas_call | solution.py:730
  7.4 1.8 %collective-permute-done.left = f32[80,128]{1,0:T(8,128)S(1)} collective-permute-done((f32[80,128]{1,0:T(8,128)S(1)}, f32[80,128]{1,0:T(8,128)S(1)}, u32[]{:S(2)}, u32[]{:S(2)}) %collective-permute-start) | collective-permute-done | bytes 40992 | tf_op jit(solution)/shard_map/ppermute | solution.py:743
  9.2 0.0 collective-permute-done.1.right
  9.2 0.1 collective-permute-start.3
  9.3 1.8 %collective-permute-start.4 = (f32[56,128]{1,0:T(8,128)S(1)}, f32[56,128]{1,0:T(8,128)S(1)}, u32[]{:S(2)}, u32[]{:S(2)}) collective-permute-start(f32[56,128]{1,0:T(8,128)S(1)} %get-tuple-element.42), channel_id=1, source_target_pairs={{8,16},{16,8},{24,0},{0,24},{9,17},{17,9},{25,1},{1,25},{10,18},{1... | collective-permute-start | bytes 86024 | tf_op jit(solution)/shard_map/ppermute | solution.py:755
  11.1 0.1 collective-permute-start.2
  11.1 0.3 %shard_map.76 = (f32[5,16,128]{2,1,0:T(8,128)S(1)}, f32[144,128]{1,0:T(8,128)S(1)}, f32[3,16,128]{2,1,0:T(8,128)S(1)}) custom-call(f32[15,16,128]{2,1,0:T(8,128)S(1)} %get-tuple-element.24.nodal, s32[48,128]{1,0:T(8,128)S(1)} %get-tuple-element.29.z_index, f32[72,128]{1,0:T(8,128)S(1)} %get-tuple-element.35.lift_in, ...), custom_call_target="tpu_custom_call" | custom-call | flops 1000000 | bytes 200000 | tf_op jit(solution)/shard_map/pallas_call | solution.py:730
  11.4 2.9 %collective-permute-done.2.far_one = f32[40,128]{1,0:T(8,128)S(1)} collective-permute-done((f32[40,128]{1,0:T(8,128)S(1)}, f32[40,128]{1,0:T(8,128)S(1)}, u32[]{:S(2)}, u32[]{:S(2)}) %collective-permute-start.2) | collective-permute-done | bytes 20512 | tf_op jit(solution)/shard_map/ppermute | solution.py:755
  14.3 0.0 collective-permute-done.4.far_two
  14.3 0.0 collective-permute-done.3.near_two
  14.3 0.9 %shard_map.77 = f32[5,16,128]{2,1,0:T(8,128)} custom-call(f32[15,16,128]{2,1,0:T(8,128)S(1)} %get-tuple-element.24.nodal, s32[48,128]{1,0:T(8,128)S(1)} %get-tuple-element.28.x_index, s32[48,128]{1,0:T(8,128)S(1)} %get-tuple-element.29.z_index, f32[9,16,128]{2,1,0:T(8,128)S(1)} %get-tuple-element.34.grad_in, f32[5,16,128]{2,1,0:T(8,128)S(1)} %get-tuple-element.36.part_in, ...), custom_call_target="tpu_custom_call" | custom-call | flops 1000000 | bytes 200000 | tf_op jit(solution)/shard_map/pallas_call | solution.py:730
  (1 shorter events, 0.0 us)
Async XLA Ops:
  1.1 8.1 %collective-permute-start = (f32[80,128]{1,0:T(8,128)S(1)}, f32[80,128]{1,0:T(8,128)S(1)}, u32[]{:S(2)}, u32[]{:S(2)}) collective-permute-start(f32[80,128]{1,0:T(8,128)S(1)} %get-tuple-element.32), channel_id=1, source_target_pairs={{0,1},{1,2},{2,3},{3,4},{4,5},{5,6},{6,7},{7,0},{8,9},{9,10},{10,1... | collective-permute-start | bytes 122888 | tf_op jit(solution)/shard_map/ppermute | solution.py:743
  4.2 5.0 %collective-permute-start.1 = (f32[80,128]{1,0:T(8,128)S(1)}, f32[80,128]{1,0:T(8,128)S(1)}, u32[]{:S(2)}, u32[]{:S(2)}) collective-permute-start(f32[80,128]{1,0:T(8,128)S(1)} %get-tuple-element.33), channel_id=1, source_target_pairs={{1,0},{2,1},{3,2},{4,3},{5,4},{6,5},{7,6},{0,7},{9,8},{10,9},{11,1... | collective-permute-start | bytes 122888 | tf_op jit(solution)/shard_map/ppermute | solution.py:744
  9.2 5.0 %collective-permute-start.3 = (f32[96,128]{1,0:T(8,128)S(1)}, f32[96,128]{1,0:T(8,128)S(1)}, u32[]{:S(2)}, u32[]{:S(2)}) collective-permute-start(f32[96,128]{1,0:T(8,128)S(1)} %get-tuple-element.41), channel_id=1, source_target_pairs={{0,8},{8,0},{16,24},{24,16},{1,9},{9,1},{17,25},{25,17},{2,10},{10... | collective-permute-start | bytes 147464 | tf_op jit(solution)/shard_map/ppermute | solution.py:755
  9.3 5.0 %collective-permute-start.4 = (f32[56,128]{1,0:T(8,128)S(1)}, f32[56,128]{1,0:T(8,128)S(1)}, u32[]{:S(2)}, u32[]{:S(2)}) collective-permute-start(f32[56,128]{1,0:T(8,128)S(1)} %get-tuple-element.42), channel_id=1, source_target_pairs={{8,16},{16,8},{24,0},{0,24},{9,17},{17,9},{25,1},{1,25},{10,18},{1... | collective-permute-start | bytes 86024 | tf_op jit(solution)/shard_map/ppermute | solution.py:755
  11.1 3.2 %collective-permute-start.2 = (f32[40,128]{1,0:T(8,128)S(1)}, f32[40,128]{1,0:T(8,128)S(1)}, u32[]{:S(2)}, u32[]{:S(2)}) collective-permute-start(f32[40,128]{1,0:T(8,128)S(1)} %get-tuple-element.40), channel_id=1, source_target_pairs={{8,16},{16,8},{24,0},{0,24},{9,17},{17,9},{25,1},{1,25},{10,18},{1... | collective-permute-start | bytes 61448 | tf_op jit(solution)/shard_map/ppermute | solution.py:755

commit v4 on v3

--- a/solution.py
+++ b/solution.py
@@ -617,9 +617,8 @@
             )
 
 
-def third_kernel(
-    nodal, x_index, z_index, grad_in, part_in, z_face, y_normal, matrix,
-    far_one, near_two, far_two, out
+def third_cover(
+    nodal, x_index, grad_in, part_in, z_face, y_normal, matrix, far_one, near_two, part_out, face_out
 ):
     cons, jac, met = split_nodal(nodal)
     frame = Frame(cons.shape[-1])
@@ -629,10 +628,8 @@
     rows = [load_rows(met, g) for g in range(3)]
     inverse = [1.0 / jac[0:8, :], 1.0 / jac[8:16, :]]
     static = far_one.shape[0]
-    got = unpack_pairs(frame, near_two.at[static:], far_two, 13)
     x_lead = x_index[40:48, :] == 1
     turned = straight(frame, unpack_pairs(frame, near_two.at[:static], far_one, 9))
-    turned = turned + turn_all(got[:9], load_indices(x_index))
     face_sign = frame.sides(-lift, lift)
 
     own = [frame.face_x(p) for p in state_f]
@@ -652,34 +649,17 @@
         ]
         slopes.append([tiles[t] * inverse[t] for t in range(2)])
     own_slopes = [frame.face_x(p) for p in slopes]
-    other_slopes = [(turned[9 + f] - face_sign * part[f]) * turned[8] for f in range(9)]
     flux_x = plain_face(own, own_prim, other, other_prim, normal_x, frame.sides(-1.0, 1.0))
     drag1 = drag_flux(own_prim[0], own_slopes, normal_x)[0]
-    drag2 = drag_flux(other_prim[0], other_slopes, normal_x)[0]
-    flux_x = [flux_x[0]] + [flux_x[1 + c] - 0.5 * (drag1[c] + drag2[c]) for c in range(4)]
-
-    edge_a = jnp.where(frame.low_half, 0, 2) + jnp.where(frame.point_row >= 2, 4, 0)
-    edge_b = edge_a + 1
-    lines = [
-        sub_gather(got[9], edge_a ^ 4),
-        sub_gather(got[9], edge_b ^ 4),
-        sub_gather(got[10], edge_a),
-        sub_gather(got[10], edge_b),
-        sub_gather(got[11], edge_a ^ 4),
-        sub_gather(got[11], edge_b ^ 4),
-        sub_gather(got[12], edge_a),
-    ]
+    flux_x = [flux_x[0]] + [flux_x[1 + c] - 0.5 * drag1[c] for c in range(4)]
+    lifts = traction([face_sign * p for p in part], normal_x)
+    stack_tiles(face_out, other_prim[0] + normal_x + lifts + [turned[8]])
+
     face = take_tiles(z_face, 0, 18)
-    lines[4:] = [lines[4 + d] + face[14 + d] for d in range(3)]
-    z_indices = load_indices(z_index)[0]
-    lines = [turn(p, z_indices) for p in lines]
-    mean = [0.5 * (a + b) for a, b in zip(face[3:7], lines[:4])]
-    edge_slopes = [face[17] * p for p in combos(mean, lines[4:])]
     normal_z = face[7:10]
     own_slopes = [frame.face_z(p) for p in slopes]
     drag1 = drag_flux(face[0:3], own_slopes, normal_z)[0]
-    drag2 = drag_flux(face[3:6], edge_slopes, normal_z)[0]
-    drag_z = [0.5 * (drag1[c] + face[10 + c] + drag2[c]) for c in range(4)]
+    drag_z = [0.5 * (drag1[c] + face[10 + c]) for c in range(4)]
 
     slopes_t = [[slopes[f][t] for f in range(9)] for t in range(2)]
     sign_y = frame.sign_lanes()
@@ -719,7 +699,56 @@
                     + row_sign * spread[t]
                 )
         for t in range(2):
-            out[c, 8 * t : 8 * t + 8, :] = -totals[t] * inverse[t]
+            part_out[c, 8 * t : 8 * t + 8, :] = -totals[t] * inverse[t]
+
+
+def edge_tiles(frame, face):
+    zero = jnp.zeros_like(face)
+    return [jnp.where(frame.low_half, face, zero), jnp.where(frame.low_half, zero, face)]
+
+
+def third_kernel(nodal, x_index, z_index, part_in, x_face, z_face, near_two, far_two, out):
+    _, jac, _ = split_nodal(nodal)
+    frame = Frame(jac.shape[-1])
+    static = near_two.shape[0] - far_two.shape[0]
+    got = unpack_pairs(frame, near_two.at[static:], far_two, 13)
+    other = take_tiles(x_face, 0, 11)
+    slopes = turn_all(got[:9], load_indices(x_index))
+    forces = traction(slopes, other[3:6])
+    forces = [other[10] * (a - b) for a, b in zip(forces, other[6:10])]
+    drag_x = drag_of(other[0:3], forces)
+
+    edge_a = jnp.where(frame.low_half, 0, 2) + jnp.where(frame.point_row >= 2, 4, 0)
+    edge_b = edge_a + 1
+    lines = [
+        sub_gather(got[9], edge_a ^ 4),
+        sub_gather(got[9], edge_b ^ 4),
+        sub_gather(got[10], edge_a),
+        sub_gather(got[10], edge_b),
+        sub_gather(got[11], edge_a ^ 4),
+        sub_gather(got[11], edge_b ^ 4),
+        sub_gather(got[12], edge_a),
+    ]
+    face = take_tiles(z_face, 0, 18)
+    lines[4:] = [lines[4 + d] + face[14 + d] for d in range(3)]
+    z_indices = load_indices(z_index)[0]
+    lines = [turn(p, z_indices) for p in lines]
+    mean = [0.5 * (a + b) for a, b in zip(face[3:7], lines[:4])]
+    edge_slopes = [face[17] * p for p in combos(mean, lines[4:])]
+    normal_z = face[7:10]
+    drag_z = drag_flux(face[3:6], edge_slopes, normal_z)[0]
+    half_sign = 0.5 * frame.sign_rows()
+    half_face = frame.sides(-0.5 * lift, 0.5 * lift)
+    for c in range(5):
+        totals = [part_in[c, 8 * t : 8 * t + 8, :] for t in range(2)]
+        if c > 0:
+            spread = frame.spread_z(drag_z[c - 1])
+            side = edge_tiles(frame, half_face * drag_x[c - 1])
+            for t in range(2):
+                scale = 1.0 / jac[8 * t : 8 * t + 8, :]
+                totals[t] = totals[t] + scale * (half_sign * spread[t] + side[t])
+        for t in range(2):
+            out[c, 8 * t : 8 * t + 8, :] = totals[t]
 
 
 def shaped(*shape, dtype=jnp.float32):
@@ -801,11 +830,15 @@
         [nodal5, shaped(144, lanes), shaped(3, nodes, lanes)],
         nodal, z_index, lift_z, left_z, right_z,
     )
+    part, x_other = call(
+        third_cover,
+        [nodal5, shaped(88, lanes)],
+        nodal, x_back, grad, part, z_face, y_normal, matrix, far_one, near_two,
+    )
     (rhs,) = call(
         third_kernel,
         [nodal5],
-        nodal, x_back, z_index, grad, part, z_face, y_normal, matrix,
-        far_one, near_two, far_two,
+        nodal, x_back, z_index, part, x_other, z_face, near_two, far_two,
     )
     return rhs.reshape(conserved.shape)
 

time: 15.3 us -> 15.5 us (1.013)
  Pallas kernels: 2.43 us -> 2.59 us
    pallas_call x5 -> x6, Pallas kernels: 2.43 us -> 2.59 us  [call(): pl.pallas_call(kernel, out_shape=outs, in_specs=in_specs or [whole] * len...]
  transfers between devices with their start and end apart: 5 -> 5, of which waited for: 2 -> 2; matrix products, arithmetic and copies ran while one was open for 0% -> 0% of each run, Pallas kernels for 3% -> 4%
where the time goes in v4:
time: 15.5 us; the launch traced here: 15.3 us
  starting transfers between devices  8.03 us (52%)
  waiting for transfers between devices  4.65 us (30%)
  Pallas kernels  2.59 us (17%)
    ppermute x1, starting transfers between devices, exchange(): lax.ppermute(low, axis, [((i + 1) % count, i) for i in range(count)])  3.1 us
    ppermute x1, starting transfers between devices, exchange(): lax.ppermute(up, axis, [(i, (i + 1) % count) for i in range(count)])  3.05 us
    ppermute x3, waiting for transfers between devices, exchange_pairs(): return lax.ppermute(values, axis, swaps)  2.89 us
    pallas_call x6, Pallas kernels, call(): pl.pallas_call(kernel, out_shape=outs, in_specs=in_specs or [whole] * len...  2.59 us
    ppermute x3, starting transfers between devices, exchange_pairs(): return lax.ppermute(values, axis, swaps)  1.88 us
    ppermute x1, waiting for transfers between devices, exchange(): lax.ppermute(up, axis, [(i, (i + 1) % count) for i in range(count)])  1.76 us
  transfers between devices with their start and end apart: 5, of which 2 were waited for; matrix products, arithmetic and copies ran while one was open for 0% of the time, Pallas kernels for 4%

profile of v4, /device:TPU:0, one launch (start us, length us, event | category | flops | bytes accessed | tf_op | source)
XLA Modules:
  0.0 15.3 jit_solution(18108703343836476203)
XLA Ops:
  0.0 1.1 %shard_map.73 = (f32[15,16,128]{2,1,0:T(8,128)S(1)}, s32[4,2,32]{2,1,0:T(2,128)S(1)}, bf16[256,384]{1,0:T(8,128)(2,1)S(1)}, s32[48,128]{1,0:T(8,128)S(1)}, f32[9...) custom-call(f32[5,16,128]{2,1,0:T(8,128)} %bitcast.9, f32[16,128]{1,0:T(8,128)} %bitcast.10, ...), custom_call_target="tpu_custom_call" | custom-call | flops 1000000 | bytes 200000 | tf_op jit(solution)/shard_map/pallas_call | solution.py:759
  1.1 3.1 %collective-permute-start = (f32[80,128]{1,0:T(8,128)S(1)}, f32[80,128]{1,0:T(8,128)S(1)}, u32[]{:S(2)}, u32[]{:S(2)}) collective-permute-start(f32[80,128]{1,0:T(8,128)S(1)} %get-tuple-element.34), channel_id=1, source_target_pairs={{0,1},{1,2},{2,3},{3,4},{4,5},{5,6},{6,7},{7,0},{8,9},{9,10},{10,1... | collective-permute-start | bytes 122888 | tf_op jit(solution)/shard_map/ppermute | solution.py:772
  4.2 3.1 %collective-permute-start.1 = (f32[80,128]{1,0:T(8,128)S(1)}, f32[80,128]{1,0:T(8,128)S(1)}, u32[]{:S(2)}, u32[]{:S(2)}) collective-permute-start(f32[80,128]{1,0:T(8,128)S(1)} %get-tuple-element.35), channel_id=1, source_target_pairs={{1,0},{2,1},{3,2},{4,3},{5,4},{6,5},{7,6},{0,7},{9,8},{10,9},{11,1... | collective-permute-start | bytes 122888 | tf_op jit(solution)/shard_map/ppermute | solution.py:773
  7.3 0.2 %shard_map.74 = (s32[48,128]{1,0:T(8,128)S(1)}, s32[48,128]{1,0:T(8,128)S(1)}, f32[72,128]{1,0:T(8,128)S(1)}, f32[40,128]{1,0:T(8,128)S(1)}, f32[40,128]{1,0:T(8,128)S(1)}) custom-call(f32[15,16,128]{2,1,0:T(8,128)S(1)} %get-tuple-element.26.nodal, s32[4,2,32]{2,1,0:T(2,128)S(1)} %get-tuple-element.27.flags, s32[48,128]{1,0:T(8,128)S(1)} %get-tuple-element.28.x_index, ...), custom_call_target="tpu_custom_call" | custom-call | flops 1000000 | bytes 200000 | tf_op jit(solution)/shard_map/pallas_call | solution.py:759
  7.4 1.8 %collective-permute-done.left = f32[80,128]{1,0:T(8,128)S(1)} collective-permute-done((f32[80,128]{1,0:T(8,128)S(1)}, f32[80,128]{1,0:T(8,128)S(1)}, u32[]{:S(2)}, u32[]{:S(2)}) %collective-permute-start) | collective-permute-done | bytes 40992 | tf_op jit(solution)/shard_map/ppermute | solution.py:772
  9.2 0.0 collective-permute-done.1.right
  9.2 0.1 collective-permute-start.3
  9.3 1.8 %collective-permute-start.4 = (f32[56,128]{1,0:T(8,128)S(1)}, f32[56,128]{1,0:T(8,128)S(1)}, u32[]{:S(2)}, u32[]{:S(2)}) collective-permute-start(f32[56,128]{1,0:T(8,128)S(1)} %get-tuple-element.46), channel_id=1, source_target_pairs={{8,16},{16,8},{24,0},{0,24},{9,17},{17,9},{25,1},{1,25},{10,18},{1... | collective-permute-start | bytes 86024 | tf_op jit(solution)/shard_map/ppermute | solution.py:784
  11.1 0.1 collective-permute-start.2
  11.1 0.3 %shard_map.76 = (f32[5,16,128]{2,1,0:T(8,128)S(1)}, f32[144,128]{1,0:T(8,128)S(1)}, f32[3,16,128]{2,1,0:T(8,128)S(1)}) custom-call(f32[15,16,128]{2,1,0:T(8,128)S(1)} %get-tuple-element.26.nodal, s32[48,128]{1,0:T(8,128)S(1)} %get-tuple-element.31.z_index, f32[72,128]{1,0:T(8,128)S(1)} %get-tuple-element.37.lift_in, ...), custom_call_target="tpu_custom_call" | custom-call | flops 1000000 | bytes 200000 | tf_op jit(solution)/shard_map/pallas_call | solution.py:759
  11.4 2.9 %collective-permute-done.2.far_one = f32[40,128]{1,0:T(8,128)S(1)} collective-permute-done((f32[40,128]{1,0:T(8,128)S(1)}, f32[40,128]{1,0:T(8,128)S(1)}, u32[]{:S(2)}, u32[]{:S(2)}) %collective-permute-start.2) | collective-permute-done | bytes 20512 | tf_op jit(solution)/shard_map/ppermute | solution.py:784
  14.3 0.0 collective-permute-done.3.near_two
  14.3 0.2 %shard_map.77 = (f32[5,16,128]{2,1,0:T(8,128)S(1)}, f32[88,128]{1,0:T(8,128)S(1)}) custom-call(f32[15,16,128]{2,1,0:T(8,128)S(1)} %get-tuple-element.26.nodal, s32[48,128]{1,0:T(8,128)S(1)} %get-tuple-element.30.x_index, f32[9,16,128]{2,1,0:T(8,128)S(1)} %get-tuple-element.36.grad_in, f32[5,16,128]{2,1,0:T(8,128)S(1)} %get-tuple-element.38.part_in, ...), custom_call_target="tpu_custom_call" | custom-call | flops 1000000 | bytes 200000 | tf_op jit(solution)/shard_map/pallas_call | solution.py:759
  14.5 0.0 collective-permute-done.4.far_two
  14.5 0.8 %shard_map.78 = f32[5,16,128]{2,1,0:T(8,128)} custom-call(f32[15,16,128]{2,1,0:T(8,128)S(1)} %get-tuple-element.26.nodal, s32[48,128]{1,0:T(8,128)S(1)} %get-tuple-element.30.x_index, s32[48,128]{1,0:T(8,128)S(1)} %get-tuple-element.31.z_index, f32[5,16,128]{2,1,0:T(8,128)S(1)} %get-tuple-element.44.part_in, f32[88,128]{1,0:T(8,128)S(1)} %get-tuple-element.45.x_face, ...), custom_call_target="tpu_custom_call" | custom-call | flops 1000000 | bytes 200000 | tf_op jit(solution)/shard_map/pallas_call | solution.py:759
  (1 shorter events, 0.0 us)
Async XLA Ops:
  1.1 8.1 %collective-permute-start = (f32[80,128]{1,0:T(8,128)S(1)}, f32[80,128]{1,0:T(8,128)S(1)}, u32[]{:S(2)}, u32[]{:S(2)}) collective-permute-start(f32[80,128]{1,0:T(8,128)S(1)} %get-tuple-element.34), channel_id=1, source_target_pairs={{0,1},{1,2},{2,3},{3,4},{4,5},{5,6},{6,7},{7,0},{8,9},{9,10},{10,1... | collective-permute-start | bytes 122888 | tf_op jit(solution)/shard_map/ppermute | solution.py:772
  4.2 5.0 %collective-permute-start.1 = (f32[80,128]{1,0:T(8,128)S(1)}, f32[80,128]{1,0:T(8,128)S(1)}, u32[]{:S(2)}, u32[]{:S(2)}) collective-permute-start(f32[80,128]{1,0:T(8,128)S(1)} %get-tuple-element.35), channel_id=1, source_target_pairs={{1,0},{2,1},{3,2},{4,3},{5,4},{6,5},{7,6},{0,7},{9,8},{10,9},{11,1... | collective-permute-start | bytes 122888 | tf_op jit(solution)/shard_map/ppermute | solution.py:773
  9.2 5.0 %collective-permute-start.3 = (f32[96,128]{1,0:T(8,128)S(1)}, f32[96,128]{1,0:T(8,128)S(1)}, u32[]{:S(2)}, u32[]{:S(2)}) collective-permute-start(f32[96,128]{1,0:T(8,128)S(1)} %get-tuple-element.43), channel_id=1, source_target_pairs={{0,8},{8,0},{16,24},{24,16},{1,9},{9,1},{17,25},{25,17},{2,10},{10... | collective-permute-start | bytes 147464 | tf_op jit(solution)/shard_map/ppermute | solution.py:784
  9.3 5.2 %collective-permute-start.4 = (f32[56,128]{1,0:T(8,128)S(1)}, f32[56,128]{1,0:T(8,128)S(1)}, u32[]{:S(2)}, u32[]{:S(2)}) collective-permute-start(f32[56,128]{1,0:T(8,128)S(1)} %get-tuple-element.46), channel_id=1, source_target_pairs={{8,16},{16,8},{24,0},{0,24},{9,17},{17,9},{25,1},{1,25},{10,18},{1... | collective-permute-start | bytes 86024 | tf_op jit(solution)/shard_map/ppermute | solution.py:784
  11.1 3.2 %collective-permute-start.2 = (f32[40,128]{1,0:T(8,128)S(1)}, f32[40,128]{1,0:T(8,128)S(1)}, u32[]{:S(2)}, u32[]{:S(2)}) collective-permute-start(f32[40,128]{1,0:T(8,128)S(1)} %get-tuple-element.42), channel_id=1, source_target_pairs={{8,16},{16,8},{24,0},{0,24},{9,17},{17,9},{25,1},{1,25},{10,18},{1... | collective-permute-start | bytes 61448 | tf_op jit(solution)/shard_map/ppermute | solution.py:784

commit v5 on v4

--- a/solution.py
+++ b/solution.py
@@ -314,24 +314,24 @@
     row4, lane4 = frame.point_row, frame.point_lane
     lane_base = frame.lane - lane4
     row_base = frame.row - row4
-    step1 = lane_base + jnp.where(swap, (lane4 - row4) & 3, lane4)
-    step2 = row_base + jnp.where(swap, (lane4 - (row4 ^ flip_b)) & 3, row4 ^ first)
-    step3 = lane_base + jnp.where(swap, ((lane4 ^ flip_a) + (row4 ^ flip_b)) & 3, lane4 ^ second)
+    step1 = row_base + jnp.where(swap, (row4 - lane4) & 3, row4 ^ first)
+    step2 = lane_base + jnp.where(swap, (row4 - (lane4 ^ flip_a)) & 3, lane4 ^ second)
+    step3 = row_base + jnp.where(swap, ((lane4 ^ flip_a) + (row4 ^ flip_b)) & 3, row4)
     return step1, step2, step3
 
 
 def turn(tile, indices):
-    return lane_gather(sub_gather(lane_gather(tile, indices[0]), indices[1]), indices[2])
-
-
-def store_indices(frame, ref, indices, master):
+    return sub_gather(lane_gather(sub_gather(tile, indices[0]), indices[1]), indices[2])
+
+
+def store_indices(ref, indices, master):
     step1, step2, step3 = indices
-    stack_tiles(ref, [step1, step2, step3, frame.swap(step1), step2 ^ 4, master])
+    stack_tiles(ref, [step1, step2, step3, step1 ^ 4, master])
 
 
 def load_indices(ref):
-    step1, step2, step3, swapped1, swapped2, _ = take_tiles(ref, 0, 6)
-    return (step1, step2, step3), (swapped1, swapped2, step3)
+    step1, step2, step3, swapped1 = take_tiles(ref, 0, 4)
+    return (step1, step2, step3), (swapped1, step2, step3)
 
 
 def turn_all(fields, both, first=0):
@@ -404,7 +404,7 @@
     x_turn = turn_indices(frame, spread_flags(frame, flags[0]), True)
     z_turn = turn_indices(frame, spread_flags(frame, flags[1]), True)
     master = spread_flags(frame, flags[2])
-    store_indices(frame, x_index, x_turn, master)
+    store_indices(x_index, x_turn, master)
     z_lead = spread_flags(frame, flags[3]) == 1
     pltpu.make_async_copy(nodal, nodal, sems.at[1]).wait()
     state = load_state(cons)
@@ -482,9 +482,9 @@
         tile = frame.face_x(load_pair(grad_in, f))
         face_out[8 * f : 8 * f + 8, :] = frame.swap(tile) if f % 2 == 0 else tile
     z_turn = turn_indices(frame, spread_flags(frame, flags[1]), False)
-    store_indices(frame, z_index, z_turn, spread_flags(frame, flags[3]))
+    store_indices(z_index, z_turn, spread_flags(frame, flags[3]))
     x_return = turn_indices(frame, spread_flags(frame, flags[0]), False)
-    store_indices(frame, x_back, x_return, take_tiles(x_index, 5, 6)[0])
+    store_indices(x_back, x_return, take_tiles(x_index, 4, 5)[0])
 
 
 def mean_of(prim1, prim2):
@@ -497,7 +497,7 @@
 ):
     cons, _, met = split_nodal(nodal)
     frame = Frame(cons.shape[-1])
-    lead = z_index[40:48, :] == 1
+    lead = z_index[32:40, :] == 1
     got = unpack(frame, left, right, 20)
     other = straight(frame, got[:9])
     own = [frame.face_z(load_pair(cons, f)) for f in range(5)]
@@ -548,7 +548,7 @@
 def second_cover(nodal, z_index, lift_in, left, right, part_out, face_out, normal_out):
     cons, _, met = split_nodal(nodal)
     frame = Frame(cons.shape[-1])
-    lead = z_index[40:48, :] == 1
+    lead = z_index[32:40, :] == 1
     both = load_indices(z_index)
     got = unpack(frame, left, right, 20)
     turned = straight(frame, got[:9])
@@ -628,7 +628,7 @@
     rows = [load_rows(met, g) for g in range(3)]
     inverse = [1.0 / jac[0:8, :], 1.0 / jac[8:16, :]]
     static = far_one.shape[0]
-    x_lead = x_index[40:48, :] == 1
+    x_lead = x_index[32:40, :] == 1
     turned = straight(frame, unpack_pairs(frame, near_two.at[:static], far_one, 9))
     face_sign = frame.sides(-lift, lift)
 
@@ -794,7 +794,7 @@
     xm, xf, zm, zf = [a.reshape(2, a.shape[-1]) for a in (x_master, x_flip, z_master, z_flip)]
     flag = (2, xm.shape[-1])
     nodal9, nodal5 = shaped(9, nodes, lanes), shaped(5, nodes, lanes)
-    index = shaped(48, lanes, dtype=jnp.int32)
+    index = shaped(40, lanes, dtype=jnp.int32)
     matrix_shape = shaped(2 * lanes, 3 * lanes, dtype=jnp.bfloat16)
     nodal, flags, matrix, x_index, grad, low_z, up_z = call(
         first_kernel,

time: 15.5 us -> 15.4 us (level)
  no operation moved by 1% of the time
where the time goes in v5:
time: 15.4 us; the launch traced here: 15.3 us
  starting transfers between devices  8.03 us (52%)
  waiting for transfers between devices  4.69 us (30%)
  Pallas kernels  2.48 us (16%)
    ppermute x1, starting transfers between devices, exchange(): lax.ppermute(low, axis, [((i + 1) % count, i) for i in range(count)])  3.1 us
    ppermute x1, starting transfers between devices, exchange(): lax.ppermute(up, axis, [(i, (i + 1) % count) for i in range(count)])  3.05 us
    ppermute x3, waiting for transfers between devices, exchange_pairs(): return lax.ppermute(values, axis, swaps)  2.92 us
    pallas_call x6, Pallas kernels, call(): pl.pallas_call(kernel, out_shape=outs, in_specs=in_specs or [whole] * len...  2.48 us
    ppermute x3, starting transfers between devices, exchange_pairs(): return lax.ppermute(values, axis, swaps)  1.88 us
    ppermute x1, waiting for transfers between devices, exchange(): lax.ppermute(up, axis, [(i, (i + 1) % count) for i in range(count)])  1.77 us
  transfers between devices with their start and end apart: 5, of which 2 were waited for; matrix products, arithmetic and copies ran while one was open for 0% of the time, Pallas kernels for 4%

profile of v5, /device:TPU:0, one launch (start us, length us, event | category | flops | bytes accessed | tf_op | source)
XLA Modules:
  0.0 15.3 jit_solution(9404421532639928396)
XLA Ops:
  0.0 1.1 %shard_map.73 = (f32[15,16,128]{2,1,0:T(8,128)S(1)}, s32[4,2,32]{2,1,0:T(2,128)S(1)}, bf16[256,384]{1,0:T(8,128)(2,1)S(1)}, s32[40,128]{1,0:T(8,128)S(1)}, f32[9...) custom-call(f32[5,16,128]{2,1,0:T(8,128)} %bitcast.9, f32[16,128]{1,0:T(8,128)} %bitcast.10, ...), custom_call_target="tpu_custom_call" | custom-call | flops 1000000 | bytes 200000 | tf_op jit(solution)/shard_map/pallas_call | solution.py:759
  1.1 3.0 %collective-permute-start = (f32[80,128]{1,0:T(8,128)S(1)}, f32[80,128]{1,0:T(8,128)S(1)}, u32[]{:S(2)}, u32[]{:S(2)}) collective-permute-start(f32[80,128]{1,0:T(8,128)S(1)} %get-tuple-element.34), channel_id=1, source_target_pairs={{0,1},{1,2},{2,3},{3,4},{4,5},{5,6},{6,7},{7,0},{8,9},{9,10},{10,1... | collective-permute-start | bytes 122888 | tf_op jit(solution)/shard_map/ppermute | solution.py:772
  4.2 3.1 %collective-permute-start.1 = (f32[80,128]{1,0:T(8,128)S(1)}, f32[80,128]{1,0:T(8,128)S(1)}, u32[]{:S(2)}, u32[]{:S(2)}) collective-permute-start(f32[80,128]{1,0:T(8,128)S(1)} %get-tuple-element.35), channel_id=1, source_target_pairs={{1,0},{2,1},{3,2},{4,3},{5,4},{6,5},{7,6},{0,7},{9,8},{10,9},{11,1... | collective-permute-start | bytes 122888 | tf_op jit(solution)/shard_map/ppermute | solution.py:773
  7.3 0.1 shard_map.74
  7.4 1.8 %collective-permute-done.left = f32[80,128]{1,0:T(8,128)S(1)} collective-permute-done((f32[80,128]{1,0:T(8,128)S(1)}, f32[80,128]{1,0:T(8,128)S(1)}, u32[]{:S(2)}, u32[]{:S(2)}) %collective-permute-start) | collective-permute-done | bytes 40992 | tf_op jit(solution)/shard_map/ppermute | solution.py:772
  9.2 0.0 collective-permute-done.1.right
  9.2 0.1 collective-permute-start.3
  9.3 1.8 %collective-permute-start.4 = (f32[56,128]{1,0:T(8,128)S(1)}, f32[56,128]{1,0:T(8,128)S(1)}, u32[]{:S(2)}, u32[]{:S(2)}) collective-permute-start(f32[56,128]{1,0:T(8,128)S(1)} %get-tuple-element.46), channel_id=1, source_target_pairs={{8,16},{16,8},{24,0},{0,24},{9,17},{17,9},{25,1},{1,25},{10,18},{1... | collective-permute-start | bytes 86024 | tf_op jit(solution)/shard_map/ppermute | solution.py:784
  11.1 0.1 collective-permute-start.2
  11.1 0.2 %shard_map.76 = (f32[5,16,128]{2,1,0:T(8,128)S(1)}, f32[144,128]{1,0:T(8,128)S(1)}, f32[3,16,128]{2,1,0:T(8,128)S(1)}) custom-call(f32[15,16,128]{2,1,0:T(8,128)S(1)} %get-tuple-element.26.nodal, s32[40,128]{1,0:T(8,128)S(1)} %get-tuple-element.31.z_index, f32[72,128]{1,0:T(8,128)S(1)} %get-tuple-element.37.lift_in, ...), custom_call_target="tpu_custom_call" | custom-call | flops 1000000 | bytes 200000 | tf_op jit(solution)/shard_map/pallas_call | solution.py:759
  11.4 2.9 %collective-permute-done.2.far_one = f32[40,128]{1,0:T(8,128)S(1)} collective-permute-done((f32[40,128]{1,0:T(8,128)S(1)}, f32[40,128]{1,0:T(8,128)S(1)}, u32[]{:S(2)}, u32[]{:S(2)}) %collective-permute-start.2) | collective-permute-done | bytes 20512 | tf_op jit(solution)/shard_map/ppermute | solution.py:784
  14.3 0.0 collective-permute-done.3.near_two
  14.3 0.2 %shard_map.77 = (f32[5,16,128]{2,1,0:T(8,128)S(1)}, f32[88,128]{1,0:T(8,128)S(1)}) custom-call(f32[15,16,128]{2,1,0:T(8,128)S(1)} %get-tuple-element.26.nodal, s32[40,128]{1,0:T(8,128)S(1)} %get-tuple-element.30.x_index, f32[9,16,128]{2,1,0:T(8,128)S(1)} %get-tuple-element.36.grad_in, f32[5,16,128]{2,1,0:T(8,128)S(1)} %get-tuple-element.38.part_in, ...), custom_call_target="tpu_custom_call" | custom-call | flops 1000000 | bytes 200000 | tf_op jit(solution)/shard_map/pallas_call | solution.py:759
  14.5 0.0 collective-permute-done.4.far_two
  14.5 0.7 %shard_map.78 = f32[5,16,128]{2,1,0:T(8,128)} custom-call(f32[15,16,128]{2,1,0:T(8,128)S(1)} %get-tuple-element.26.nodal, s32[40,128]{1,0:T(8,128)S(1)} %get-tuple-element.30.x_index, s32[40,128]{1,0:T(8,128)S(1)} %get-tuple-element.31.z_index, f32[5,16,128]{2,1,0:T(8,128)S(1)} %get-tuple-element.44.part_in, f32[88,128]{1,0:T(8,128)S(1)} %get-tuple-element.45.x_face, ...), custom_call_target="tpu_custom_call" | custom-call | flops 1000000 | bytes 200000 | tf_op jit(solution)/shard_map/pallas_call | solution.py:759
  (1 shorter events, 0.0 us)
Async XLA Ops:
  1.1 8.1 %collective-permute-start = (f32[80,128]{1,0:T(8,128)S(1)}, f32[80,128]{1,0:T(8,128)S(1)}, u32[]{:S(2)}, u32[]{:S(2)}) collective-permute-start(f32[80,128]{1,0:T(8,128)S(1)} %get-tuple-element.34), channel_id=1, source_target_pairs={{0,1},{1,2},{2,3},{3,4},{4,5},{5,6},{6,7},{7,0},{8,9},{9,10},{10,1... | collective-permute-start | bytes 122888 | tf_op jit(solution)/shard_map/ppermute | solution.py:772
  4.2 5.0 %collective-permute-start.1 = (f32[80,128]{1,0:T(8,128)S(1)}, f32[80,128]{1,0:T(8,128)S(1)}, u32[]{:S(2)}, u32[]{:S(2)}) collective-permute-start(f32[80,128]{1,0:T(8,128)S(1)} %get-tuple-element.35), channel_id=1, source_target_pairs={{1,0},{2,1},{3,2},{4,3},{5,4},{6,5},{7,6},{0,7},{9,8},{10,9},{11,1... | collective-permute-start | bytes 122888 | tf_op jit(solution)/shard_map/ppermute | solution.py:773
  9.2 5.0 %collective-permute-start.3 = (f32[96,128]{1,0:T(8,128)S(1)}, f32[96,128]{1,0:T(8,128)S(1)}, u32[]{:S(2)}, u32[]{:S(2)}) collective-permute-start(f32[96,128]{1,0:T(8,128)S(1)} %get-tuple-element.43), channel_id=1, source_target_pairs={{0,8},{8,0},{16,24},{24,16},{1,9},{9,1},{17,25},{25,17},{2,10},{10... | collective-permute-start | bytes 147464 | tf_op jit(solution)/shard_map/ppermute | solution.py:784
  9.3 5.2 %collective-permute-start.4 = (f32[56,128]{1,0:T(8,128)S(1)}, f32[56,128]{1,0:T(8,128)S(1)}, u32[]{:S(2)}, u32[]{:S(2)}) collective-permute-start(f32[56,128]{1,0:T(8,128)S(1)} %get-tuple-element.46), channel_id=1, source_target_pairs={{8,16},{16,8},{24,0},{0,24},{9,17},{17,9},{25,1},{1,25},{10,18},{1... | collective-permute-start | bytes 86024 | tf_op jit(solution)/shard_map/ppermute | solution.py:784
  11.1 3.2 %collective-permute-start.2 = (f32[40,128]{1,0:T(8,128)S(1)}, f32[40,128]{1,0:T(8,128)S(1)}, u32[]{:S(2)}, u32[]{:S(2)}) collective-permute-start(f32[40,128]{1,0:T(8,128)S(1)} %get-tuple-element.42), channel_id=1, source_target_pairs={{8,16},{16,8},{24,0},{0,24},{9,17},{17,9},{25,1},{1,25},{10,18},{1... | collective-permute-start | bytes 61448 | tf_op jit(solution)/shard_map/ppermute | solution.py:784
